TPU v7x, 256 devices: a whole 4x4x8 slice. The times are simulated.
256 devices in a mesh: context: 32 (over z, x), ulysses: 4 (over y), dp: 2 (over core).
Axes of the slice: x: 4, y: 4, z: 8, core: 2. Of those that a mesh axis runs over, the one named last changes fastest.
Arguments:
- queries: bfloat16 [32768, 4096], P(('dp', 'context', 'ulysses')), parts along dimension 0, may hold values from -5 to 5
- keys: bfloat16 [32768, 512], P(('dp', 'context', 'ulysses')), parts along dimension 0, may hold values from -5 to 5
- values: bfloat16 [32768, 512], P(('dp', 'context', 'ulysses')), parts along dimension 0, may hold values from -6 to 6
- segments: int32 [32768], P(('dp', 'context')), parts along dimension 0, may hold values from 0 to 63, never falling along the last dimension, each value on 1 to 4096 neighbouring positions
- feat_q: bfloat16 [32, 128, 128], P('ulysses'), may hold values from -2 to 2
- feat_k: bfloat16 [4, 128, 128], P('ulysses'), may hold values from -2 to 2
Outputs:
- error: bfloat16 [32768, 4096], P(('dp', 'context'), 'ulysses'), parts along dimension 0
- grad_keys: bfloat16 [32768, 512], P(('dp', 'context'), 'ulysses'), parts along dimension 0
- grad_feat_q: float32 [64, 128, 128], P(('dp', 'ulysses')), parts along dimension 0
- grad_feat_k: float32 [8, 128, 128], P(('dp', 'ulysses')), parts along dimension 0
There are 2 independent parts, one for each index of `dp`. A program takes and returns all parts, laid end to end along the dimension named above; an argument that names none is the same for every part. Nothing has to cross between parts.
Inputs may be any that keep to these rules, and one draw needn't show every extreme that they name: `segments`: document numbers never fall along the sequence; each document covers 1 to 4096 positions, and one covers exactly 4096.
All inputs are finite; a program needn't handle non-finite values.
Results may differ from a plain program's by a relative error of at most 0.015.
Values may be sent and summed in bfloat16 or wider, within the bound.
A program may use at most 128 MiB of HBM per device.

v0:
```python
import math

import jax
import jax.numpy as jnp
from jax import lax
from jax.sharding import PartitionSpec as P

WIN = 128


def entering(value, axis, join, neutral, backward):
    count, mine = (lax.axis_size(axis), lax.axis_index(axis))
    pieces = jax.tree.map(lambda part: lax.all_gather(part, axis), value)
    if backward:
        pieces = jax.tree.map(lambda part: part[::-1], pieces)
        mine = count - 1 - mine
    so_far = jax.tree.map(
        lambda part, zero: jnp.full_like(part, 0) + jnp.asarray(zero, part.dtype), value, neutral
    )

    def lap(position, so_far):
        longer = join(so_far, jax.tree.map(lambda part: part[position], pieces))
        return jax.tree.map(lambda new, old: jnp.where(position < mine, new, old), longer, so_far)

    return lax.fori_loop(0, count - 1, lap, so_far)


def from_behind(block, axis, distance):
    devices = range(lax.axis_size(axis))
    route = [(i - distance, i) for i in devices if i - distance in devices]
    return lax.ppermute(block, axis, route)


def feature_map(pre):
    return jnp.where(pre > 0, pre + 1.0, jnp.exp(jnp.minimum(pre, 0.0)))


def feature_slope(pre):
    return jnp.where(pre > 0, 1.0, jnp.exp(jnp.minimum(pre, 0.0)))


def join_parts(earlier, later):
    empty_later = later[2] < 0
    keep = (earlier[2] == later[2]) | empty_later
    return (
        later[0] + jnp.where(keep, earlier[0], 0.0),
        later[1] + jnp.where(keep, earlier[1], 0.0),
        jnp.where(empty_later, earlier[2], later[2]),
    )


def widened(form, left, right):
    return jnp.einsum(form, left, right, preferred_element_type=jnp.float32)


def split_pair(whole):
    upper = whole.astype(jnp.bfloat16)
    lower = (whole - upper.astype(jnp.float32)).astype(jnp.bfloat16)
    return (upper, lower)


def paired(form, left, pair, pair_first):
    if pair_first:
        return widened(form, pair[0], left) + widened(form, pair[1], left)
    return widened(form, left, pair[0]) + widened(form, left, pair[1])


def on_device(queries, keys, values, segments, feat_q, feat_k):
    query_all, key_all, value_all = (
        lax.all_to_all(queries, "ulysses", split_axis=1, concat_axis=0, tiled=True),
        lax.all_to_all(keys, "ulysses", split_axis=1, concat_axis=0, tiled=True),
        lax.all_to_all(values, "ulysses", split_axis=1, concat_axis=0, tiled=True),
    )
    length = query_all.shape[0]
    kv_heads, width, feats = feat_k.shape
    group = feat_q.shape[0] // kv_heads
    query_heads = query_all.reshape(length, kv_heads, group, width)
    key_heads = key_all.reshape(length, kv_heads, width)
    value_heads = value_all.reshape(length, kv_heads, width)
    pre_q = widened("rgke,gkef->rgkf", query_heads, feat_q.reshape(kv_heads, group, width, feats))
    phi_q = feature_map(pre_q).astype(jnp.bfloat16)
    pre_k = widened("rge,gef->rgf", key_heads, feat_k)
    phi_k = feature_map(pre_k).astype(jnp.bfloat16)
    here = lax.axis_index("context")
    first_id = segments[0]
    last_id = segments[length - 1]
    tail_k = jnp.where((segments == last_id)[:, None, None], phi_k, jnp.zeros_like(phi_k))
    state_local = widened("rgf,rge->gfe", tail_k, value_heads)
    norm_local = jnp.sum(tail_k.astype(jnp.float32), axis=0)
    blank = (jnp.zeros_like(state_local), jnp.zeros_like(norm_local))
    state_in, norm_in, state_id = entering(
        (state_local, norm_local, last_id),
        "context",
        join_parts,
        (blank[0], blank[1], jnp.int32(-1)),
        False,
    )
    state_parts = split_pair(state_in)
    norm_parts = split_pair(norm_in)
    rim_keys, rim_values, rim_ids = from_behind(
        (key_heads[length - WIN :], value_heads[length - WIN :], segments[length - WIN :]),
        "context",
        1,
    )
    rim_ids = jnp.where(here > 0, rim_ids, -1)
    keys_ext = jnp.concatenate([rim_keys, key_heads], axis=0)
    values_ext = jnp.concatenate([rim_values, value_heads], axis=0)
    ids_ext = jnp.concatenate([rim_ids, segments], axis=0)
    place = jnp.arange(length)
    place_ext = jnp.arange(length + WIN) - WIN
    take_in = segments == state_id
    first_rows = segments == first_id
    inv_scale = 1.0 / math.sqrt(width)
    block = min(512, length)
    cot_state = blank[0]
    cot_norm = blank[1]
    linked = (place[None, :] <= place[:, None]) & (segments[None, :] == segments[:, None])
    linked = linked[:, None, None, :]
    scores = jnp.where(linked, widened("igkf,jgf->igkj", phi_q, phi_k), 0.0)
    carried = take_in[:, None, None]
    numer = widened("igkj,jge->igke", scores.astype(jnp.bfloat16), value_heads) + jnp.where(
        carried[..., None], paired("igkf,gfe->igke", phi_q, state_parts, False), 0.0
    )
    denom = jnp.sum(scores, axis=-1) + jnp.where(
        carried, paired("igkf,gf->igk", phi_q, norm_parts, False), 0.0
    )
    student = numer / denom[..., None]
    seen = (
        (place_ext[None, :] <= place[:, None])
        & (place_ext[None, :] > place[:, None] - WIN)
        & (ids_ext[None, :] == segments[:, None])
    )
    logits = jnp.where(
        seen[:, None, None, :],
        widened("igke,jge->igkj", query_heads, keys_ext) * inv_scale,
        -jnp.inf,
    )
    top = jnp.max(logits, axis=-1, keepdims=True)
    probs = jnp.exp(logits - top)
    teacher = (
        widened("igkj,jge->igke", probs.astype(jnp.bfloat16), values_ext)
        / jnp.sum(probs, axis=-1)[..., None]
    )
    gap = student - teacher
    errors = gap.astype(jnp.bfloat16).reshape(block, kv_heads * group * width)
    upstream = 32.0 * gap
    d_numer = (upstream / denom[..., None]).astype(jnp.bfloat16)
    d_denom = -jnp.sum(upstream * student, axis=-1) / denom
    d_scores = jnp.where(
        linked, widened("igke,jge->igkj", d_numer, value_heads) + d_denom[..., None], 0.0
    ).astype(jnp.bfloat16)
    d_phi_q_parts = widened("igkj,jgf->igkf", d_scores, phi_k) + jnp.where(
        carried[..., None],
        paired("gfe,igke->igkf", d_numer, state_parts, True)
        + d_denom[..., None] * norm_in[None, :, None, :],
        0.0,
    )
    d_phi_k = widened("igkj,igkf->jgf", d_scores, phi_q)
    head_rows = first_rows[:, None, None, None]
    cot_state = widened(
        "igkf,igke->gfe", jnp.where(head_rows, phi_q, jnp.zeros_like(phi_q)), d_numer
    )
    cot_norm = jnp.sum(jnp.where(head_rows, d_denom[..., None] * phi_q, 0.0), axis=(0, 2))
    back_state, back_norm, back_id = entering(
        (cot_state, cot_norm, first_id),
        "context",
        join_parts,
        (blank[0], blank[1], jnp.int32(-1)),
        True,
    )
    take_back = (segments == back_id)[:, None, None]
    back_parts = split_pair(back_state)
    d_phi_k = d_phi_k + jnp.where(
        take_back, paired("gfe,jge->jgf", value_heads, back_parts, True) + back_norm[None], 0.0
    )
    d_pre_k = (d_phi_k * feature_slope(pre_k)).astype(jnp.bfloat16)
    grad_keys = (
        widened("jgf,gef->jge", d_pre_k, feat_k)
        .astype(jnp.bfloat16)
        .reshape(length, kv_heads * width)
    )
    d_pre_q = (d_phi_q_parts * feature_slope(pre_q)).astype(jnp.bfloat16)
    grad_query_maps = widened("rgke,rgkf->gkef", query_heads, d_pre_q).reshape(
        kv_heads * group, width, feats
    )
    grad_key_maps = widened("rge,rgf->gef", key_heads, d_pre_k)
    grad_query_maps, grad_key_maps = (
        lax.psum(grad_query_maps.astype(jnp.bfloat16), "context").astype(jnp.float32),
        lax.psum(grad_key_maps.astype(jnp.bfloat16), "context").astype(jnp.float32),
    )
    scale = 1.0 / math.sqrt(length * lax.axis_size("context"))
    return (errors, grad_keys, grad_query_maps * scale, grad_key_maps * scale)


def solution(mesh):
    in_specs = (
        P(("dp", "context", "ulysses"), None),
        P(("dp", "context", "ulysses"), None),
        P(("dp", "context", "ulysses"), None),
        P(("dp", "context")),
        P("ulysses", None, None),
        P("ulysses", None, None),
    )
    out_specs = (
        P(("dp", "context"), "ulysses"),
        P(("dp", "context"), "ulysses"),
        P(("dp", "ulysses"), None, None),
        P(("dp", "ulysses"), None, None),
    )
    return jax.shard_map(
        on_device, mesh=mesh, in_specs=in_specs, out_specs=out_specs, check_vma=False
    )
```

profile of v0, /device:TPU:2, one launch (start us, length us, event | category | flops | bytes accessed | tf_op | source)
XLA Modules:
  0.0 717.6 jit_solution(18378612023101309730)
XLA Ops:
  9.1 4.5 all-to-all-start
  14.8 1.9 fusion.127
  19.7 4.8 all-to-all-start.2
  26.2 4.3 all-to-all-done.2
  32.4 3.5 all-to-all-start.1
  36.0 3.4 collective-permute-start.1
  40.4 21.6 %all-reduce.2 = (s32[32]{0:T(128)S(1)}, s32[32]{0:T(128)}) all-reduce(s32[32]{0:T(128)S(1)} %get-tuple-element.424, s32[32]{0:T(128)S(1)} %slice_dynamic-update-slice_fusion), channel_id=1, replica_groups=mesh['context'=32,'ulysses'=4,'dp'=2] {'context'}, use_global_device_ids=true, to_apply=%add | all-reduce | flops 64 | bytes 512
  64.0 3.3 collective-permute-start.2
  67.9 4.0 collective-permute-start
  71.9 37.9 %all-gather.4 = f32[32,1,128]{2,1,0:T(1,128)S(1)} all-gather(f32[1,1,128]{2,1,0:T(1,128)S(1)} %bitcast.397), channel_id=3, replica_groups=mesh['context'=32,'ulysses'=4,'dp'=2] {'context'}, dimensions={0}, use_global_device_ids=true | all-gather | bytes 16896 | tf_op jit(solution)/shard_map/all_gather | solution.py:13
  110.0 2.0 select_convert_fusion
  112.0 4.0 fusion.10
  116.1 1.8 fusion.9
  117.9 4.0 copy-done.1
  121.9 2.2 fusion.4
  124.1 107.3 %while.36 = (s32[]{:T(128)}, f32[1,128,128]{2,1,0:T(8,128)S(1)}, f32[1,128]{1,0:T(1,128)S(1)}, s32[]{:T(128)}, s32[]{:T(128)}, /*index=5*/f32[32,1,128,128]{3,2,...) while((s32[]{:T(128)}, f32[1,128,128]{2,1,0:T(8,128)S(1)}, ...), condition=%wide.region_2.3_spmd.clone, body=%wide.region_1.2_spmd.clone.sunk | while | flops 66057 | bytes 198336 | solution.py:25
  231.9 1.9 fusion.51
  233.8 1.8 fusion.55
  235.6 1.8 fusion.57
  238.0 2.4 copy.112
  241.8 4.7 fusion.24
  247.8 4.8 multiply_reduce_fusion
  252.6 1.8 fusion.44
  256.1 2.1 fusion.84
  258.7 5.2 fusion.39
  265.6 36.2 %all-gather.5 = f32[32,1,128]{2,1,0:T(1,128)S(1)} all-gather(f32[1,1,128]{2,1,0:T(1,128)S(1)} %bitcast.396), channel_id=5, replica_groups=mesh['context'=32,'ulysses'=4,'dp'=2] {'context'}, dimensions={0}, use_global_device_ids=true | all-gather | bytes 16896 | tf_op jit(solution)/shard_map/all_gather | solution.py:13
  301.8 2.3 copy.100
  304.0 102.3 %all-reduce.5.cloned.1.call-done = bf16[8,128,128]{1,2,0:T(8,128)(2,1)} async-done(((bf16[8,128,128]{1,2,0:T(8,128)(2,1)}), bf16[8,128,128]{1,2,0:T(8,128)(2,1)}) %all-reduce.5.cloned.1.call-update) | async-done | bytes 262160 | tf_op jit(solution)/shard_map/psum | solution.py:188
  408.3 76.1 %all-gather.11.cloned.1.call-done = f32[4096,128]{1,0:T(8,128)} async-done(((f32[128,128]{1,0:T(8,128)}), f32[4096,128]{1,0:T(8,128)}) %all-gather.11.cloned.1.call-update) | async-done | bytes 2097168 | tf_op jit(solution)/shard_map/all_gather | solution.py:13
  486.1 81.0 %while.37 = (s32[]{:T(128)}, f32[1,128,128]{2,1,0:T(8,128)S(1)}, f32[1,128]{1,0:T(1,128)S(1)}, s32[]{:T(128)}, s32[]{:T(128)}, /*index=5*/f32[32,1,128,128]{3,2,...) while((s32[]{:T(128)}, f32[1,128,128]{2,1,0:T(8,128)S(1)}, ...), condition=%wide.region_9.10_spmd.clone, body=%wide.region_8.9_spmd.clone.sunk | while | flops 66057 | bytes 198336 | solution.py:25
  569.3 3.7 fusion.41
  574.1 136.2 %psum.15 = bf16[1,128,128]{1,2,0:T(8,128)(2,1)S(1)} all-reduce(bf16[1,128,128]{1,2,0:T(8,128)(2,1)S(1)} %fusion.42), channel_id=1, replica_groups=mesh['context'=32,'ulysses'=4,'dp'=2] {'context'}, use_global_device_ids=true, to_apply=%region_11.12 | all-reduce | flops 16384 | bytes 65536 | tf_op jit(solution)/shard_map/psum | solution.py:189
  (296 shorter events, 93.7 us)
Async XLA Ops:
  7.2 102.9 %copy-start = (bf16[8,128,128]{2,1,0:T(8,128)(2,1)S(1)}, bf16[8,128,128]{2,1,0:T(8,128)(2,1)}, u32[]{:S(2)}) copy-start(bf16[8,128,128]{2,1,0:T(8,128)(2,1)} %param.14) | copy-start | bytes 786436
  7.2 24.2 %copy-start.13 = (bf16[128,4096]{1,0:T(8,128)(2,1)S(1)}, bf16[128,4096]{1,0:T(8,128)(2,1)}, u32[]{:S(2)}) copy-start(bf16[128,4096]{1,0:T(8,128)(2,1)} %param.10) | copy-start | bytes 3145732
  9.1 10.6 %all-to-all-start = ((bf16[128,4,128]{2,0,1:T(8,128)(2,1)}), bf16[128,4,128]{2,0,1:T(8,128)(2,1)S(1)}, u32[]{:S(2)}, u32[]{:S(2)}) async-start(bf16[128,4,128]{2,0,1:T(8,128)(2,1)} %copy.71), calls=%async_computation | async-start | bytes 262144 | tf_op jit(solution)/shard_map/all_to_all | solution.py:71
  19.7 96.3 %copy-start.11 = (bf16[128,4,128]{2,0,1:T(8,128)(2,1)}, bf16[128,4,128]{2,0,1:T(8,128)(2,1)S(1)}, u32[]{:S(2)}) copy-start(bf16[128,4,128]{2,0,1:T(8,128)(2,1)S(1)} %all-to-all-done) | copy-start | bytes 393220
  19.7 10.8 %all-to-all-start.2 = ((bf16[128,4,128]{0,2,1:T(8,128)(2,1)}), bf16[128,4,128]{0,2,1:T(8,128)(2,1)S(1)}, u32[]{:S(2)}, u32[]{:S(2)}) async-start(bf16[128,4,128]{0,2,1:T(8,128)(2,1)} %bitcast.15), calls=%async_computation.2 | async-start | bytes 262144 | tf_op jit(solution)/shard_map/all_to_all | solution.py:72
  24.5 99.5 %all-gather.9.cloned.1.call-start = ((), (), s32[]{:S(2)}) async-start(), calls=%async_computation.4 | async-start | bytes 2162688 | tf_op jit(solution)/shard_map/all_gather | solution.py:13
  26.2 85.8 %copy-start.16 = (bf16[128,512]{1,0:T(8,128)(2,1)}, bf16[128,512]{1,0:T(8,128)(2,1)S(1)}, u32[]{:S(2)}) copy-start(bf16[128,512]{1,0:T(8,128)(2,1)S(1)} %get-tuple-element.417) | copy-start | bytes 393220
  30.5 36.8 %copy-start.9 = (bf16[128,4,128]{0,2,1:T(8,128)(2,1)}, bf16[128,4,128]{0,2,1:T(8,128)(2,1)S(1)}, u32[]{:S(2)}) copy-start(bf16[128,4,128]{0,2,1:T(8,128)(2,1)S(1)} %all-to-all-done.2) | copy-start | bytes 393220
  31.4 4.6 copy-start.19
  32.4 77.3 %all-to-all-start.1 = ((bf16[128,4,1024]{2,0,1:T(8,128)(2,1)}), bf16[128,4,1024]{2,0,1:T(8,128)(2,1)S(1)}, u32[]{:S(2)}, u32[]{:S(2)}) async-start(bf16[128,4,1024]{2,0,1:T(8,128)(2,1)} %bitcast.364), calls=%async_computation.1 | async-start | bytes 2097152 | tf_op jit(solution)/shard_map/all_to_all | solution.py:70
  36.0 370.3 %all-reduce.5.cloned.1.call-start = ((), (), s32[]{:S(2)}) async-start(), calls=%async_computation.3 | async-start | bytes 524288 | tf_op jit(solution)/shard_map/psum | solution.py:188
  36.0 26.0 %collective-permute-start.1 = (s32[128]{0:T(128)S(1)}, s32[128]{0:T(128)S(1)}, u32[]{:S(2)}, u32[]{:S(2)}) collective-permute-start(s32[128]{0:T(128)S(1)} %slice.24), channel_id=1, source_target_pairs={{0,8},{8,16},{16,24},{24,32},{32,40},{40,48},{48,56},{56,64},{64,7... | collective-permute-start | bytes 1544 | tf_op jit(solution)/shard_map/ppermute | solution.py:31
  40.4 71.7 %copy-start.14 = (pred[512,512]{0,1:T(8,128)(4,1)}, pred[512,512]{0,1:T(8,128)(4,1)S(1)}, u32[]{:S(2)}) copy-start(pred[512,512]{0,1:T(8,128)(4,1)S(1)} %fusion.66) | copy-start | bytes 786436
  62.5 55.4 %copy-start.7 = (pred[512,640]{0,1:T(8,128)(4,1)}, pred[512,640]{0,1:T(8,128)(4,1)S(1)}, u32[]{:S(2)}) copy-start(pred[512,640]{0,1:T(8,128)(4,1)S(1)} %fusion.31) | copy-start | bytes 983044
  64.0 52.1 %collective-permute-start.2 = (bf16[128,1,128]{2,0,1:T(8,128)(2,1)S(1)}, bf16[128,1,128]{2,0,1:T(8,128)(2,1)S(1)}, u32[]{:S(2)}, u32[]{:S(2)}) collective-permute-start(bf16[128,1,128]{2,0,1:T(8,128)(2,1)S(1)} %slice_bitcast_fusion), channel_id=1, source_target_pairs={{0,8},{8,16},{16,24},{24,32},{32,40},{40,48},{48,56},{56,64},{64,7... | collective-permute-start | bytes 98312 | tf_op jit(solution)/shard_map/ppermute | solution.py:31
  67.9 178.6 %collective-permute-start = (bf16[128,1,128]{0,2,1:T(8,128)(2,1)}, bf16[128,1,128]{0,2,1:T(8,128)(2,1)}, u32[]{:S(2)}, u32[]{:S(2)}) collective-permute-start(bf16[128,1,128]{0,2,1:T(8,128)(2,1)} %slice_bitcast_fusion.1), channel_id=1, source_target_pairs={{0,8},{8,16},{16,24},{24,32},{32,40},{40,48},{48,56},{56,64},{64,7... | collective-permute-start | bytes 98312 | tf_op jit(solution)/shard_map/ppermute | solution.py:31
  110.0 6.1 copy-start.2
  117.9 4.0 copy-start.1
  238.0 8.5 %slice-start = ((s8[10485760]{0:T(1024)(128)(4,1)}), s8[2097152]{0:T(1024)(128)(4,1)S(1)}, s32[]{:S(2)}) async-start(s8[10485760]{0:T(1024)(128)(4,1)} %bitcast.377), calls=%async_computation.6 | async-start | bytes 4194304
  241.7 4.8 slice-start.1
  241.7 6.0 slice-start.2
  241.7 6.0 copy-start.8
  241.8 6.0 copy-start.18
  252.6 3.5 copy-start.5
  252.6 1.8 copy-start.10
  252.6 1.8 copy-start.15
  256.1 2.6 copy-start.4
  256.1 2.6 copy-start.3
  258.7 5.3 copy-start.6
  263.9 220.4 %all-gather.11.cloned.1.call-start = ((), (), s32[]{:S(2)}) async-start(), calls=%async_computation.5 | async-start | bytes 2162688 | tf_op jit(solution)/shard_map/all_gather | solution.py:13
  569.3 3.7 copy-start.12
  569.3 3.9 copy-start.20
  (2 other events, 2.9 us)
Sparse Core Ops, SparseCore 0:
  31.5 77.6 all-gather.8
  264.1 142.1 all-reduce.4
  409.5 74.8 all-gather.10
where the time goes:
time: 727 us; the launch traced here: 718 us
  blocking collectives  232 us (32%)
  waiting for transfers between devices  183 us (25%)
  loops' own time  123 us (17%)
  local copies, waits for them, and re-layouts  61.8 us (9%)
  matrix products  44.6 us (6%)
  other arithmetic  35.4 us (5%)
  starting transfers between devices  23.5 us (3%)
  between operations  14.2 us (2%)
    psum x1, blocking collectives, on_device(): lax.psum(grad_key_maps.astype(jnp.bfloat16), 'context').astype(jnp.float32)  136 us
    another operation x2, loops' own time, entering(): return lax.fori_loop(0, count - 1, lap, so_far)  123 us
    psum x1, waiting for transfers between devices, on_device(): lax.psum(grad_query_maps.astype(jnp.bfloat16), 'context')  102 us
    all_gather x2, waiting for transfers between devices, entering(): pieces = jax.tree.map(lambda part: lax.all_gather(part, axis), value)  76.1 us
    all_gather x2, blocking collectives, entering(): pieces = jax.tree.map(lambda part: lax.all_gather(part, axis), value)  74 us
    dot_general x21, matrix products, widened(): return jnp.einsum(form, left, right, preferred_element_type=jnp.float32)  44.6 us
    dynamic_slice x62, local copies, waits for them, and re-layouts, lap(): longer = join(so_far, jax.tree.map(lambda part: part[position], pieces))  36.4 us
    select_n x124, other arithmetic, lap(): jnp.where(position < mine, new, old)  28.5 us
  transfers between devices with their start and end apart: 9, of which 3 were waited for; matrix products, arithmetic and copies ran while one was open for 12% of the time, Pallas kernels for 0%

commit v1 on v0

v1 whole, which is shorter than its diff:
```python
import functools
import math

import jax
import jax.numpy as jnp
from jax import lax
from jax.experimental import pallas as pl
from jax.experimental.pallas import tpu as pltpu
from jax.sharding import PartitionSpec as P

WIN = 128
REACH = 8
TAIL = 16
MESH = pl.DeviceIdType.MESH
F32 = jnp.float32
BF16 = jnp.bfloat16


def dot_nn(a, b):
    return lax.dot_general(a, b, (((1,), (0,)), ((), ())), preferred_element_type=F32)


def dot_nt(a, b):
    return lax.dot_general(a, b, (((1,), (1,)), ((), ())), preferred_element_type=F32)


def dot_tn(a, b):
    return lax.dot_general(a, b, (((0,), (0,)), ((), ())), preferred_element_type=F32)


def remote(src, dst, send, recv, **where):
    return pltpu.make_async_remote_copy(
        src_ref=src, dst_ref=dst, send_sem=send, recv_sem=recv, device_id=where, device_id_type=MESH
    )


def whole(ref, sem):
    return pltpu.make_async_copy(ref, ref, sem)


def columns_of(seg_row):
    length = seg_row.shape[1]
    parts = [
        jnp.transpose(jnp.broadcast_to(seg_row[:, i : i + 128].astype(F32), (128, 128)))
        for i in range(0, length, 128)
    ]
    return jnp.concatenate(parts, axis=0)


def payload(state, norm, ident):
    row = lax.broadcasted_iota(jnp.int32, (TAIL, norm.shape[1]), 0)
    tail = jnp.where(row == 0, norm, jnp.where(row == 1, ident, 0.0))
    return state.astype(BF16), tail.astype(BF16)


def gathered(buf, ident, here, count, forward):
    feats = buf.shape[1] - TAIL
    state = jnp.zeros((feats, buf.shape[2]), F32)
    norm = jnp.zeros((1, buf.shape[2]), F32)
    for k in range(REACH):
        inside = here > k if forward else here + k + 1 < count
        tail = buf[k, feats : feats + TAIL, :].astype(F32)
        keep = (tail[1:2, :] == ident) & inside
        state += jnp.where(keep, buf[k, 0:feats, :].astype(F32), 0.0)
        norm += jnp.where(keep, tail[0:1, :], 0.0)
    return state, norm


def enter_kernel(
    q_ref, k_ref, v_ref, seg_ref, fk_ref,
    q_out, kx_out, vx_out, rim_out, phi_out, slope_out, state_out, norm_out,
    sbuf, rbuf, rim_in, qs, ks, vs, qr, kr, vr, rs, rr, xs, xr,
):
    here, mine = lax.axis_index("context"), lax.axis_index("ulysses")
    count, split = lax.axis_size("context"), lax.axis_size("ulysses")
    rows = k_ref.shape[0]
    wide, thin = q_out.shape[1], kx_out.shape[1]
    length = rows * split

    barrier = pltpu.get_barrier_semaphore()
    for j in range(1, split):
        pl.semaphore_signal(
            barrier, inc=1, device_id={"ulysses": lax.rem(mine + j, split)}, device_id_type=MESH
        )
    for k in range(1, REACH + 1):
        for other in (lax.rem(here + k, count), lax.rem(here + count - k, count)):
            pl.semaphore_signal(barrier, inc=1, device_id={"context": other}, device_id_type=MESH)

    def piece(ref, who, size):
        return ref.at[:, pl.ds(pl.multiple_of(who * size, 128), size)]

    def place(ref, start):
        return ref.at[pl.ds(pl.multiple_of(start + mine * rows, 128), rows), :]

    jobs = (
        (k_ref, kx_out, thin, WIN, ks, kr),
        (v_ref, vx_out, thin, WIN, vs, vr),
        (q_ref, q_out, wide, 0, qs, qr),
    )
    for src, dst, size, start, _, recv in jobs:
        pltpu.make_async_copy(piece(src, mine, size), place(dst, start), recv).start()
    pl.semaphore_wait(barrier, split - 1 + 2 * REACH)

    sends = []
    for src, dst, size, start, send, recv in jobs:
        for j in range(1, split):
            peer = lax.rem(mine + j, split)
            copy = remote(
                piece(src, peer, size), place(dst, start), send.at[j - 1], recv, ulysses=peer
            )
            copy.start()
            sends.append(copy)

    whole(kx_out.at[pl.ds(WIN, length), :], kr).wait()
    whole(vx_out.at[pl.ds(WIN, length), :], vr).wait()
    after = lax.rem(here + 1, count)
    edge = pl.ds(length, WIN)
    rims = [
        remote(kx_out.at[edge, :], kx_out.at[pl.ds(0, WIN), :], rs.at[0], rr.at[0], context=after),
        remote(vx_out.at[edge, :], vx_out.at[pl.ds(0, WIN), :], rs.at[1], rr.at[1], context=after),
        remote(seg_ref.at[:, pl.ds(length - WIN, WIN)], rim_in, rs.at[2], rr.at[2], context=after),
    ]
    for copy in rims:
        copy.start()

    seg_row = seg_ref[...]
    seg_col = columns_of(seg_row)
    last_id = jnp.max(seg_row, axis=1, keepdims=True).astype(F32)
    first_id = jnp.min(seg_row, axis=1, keepdims=True).astype(F32)
    pre = dot_nn(kx_out[WIN : WIN + length, :], fk_ref[...])
    small = jnp.exp(jnp.minimum(pre, 0.0))
    phi = jnp.where(pre > 0, pre + 1.0, small)
    phi_out[...] = phi.astype(BF16)
    slope_out[...] = jnp.where(pre > 0, 1.0, small)
    tail = jnp.where(seg_col == last_id, phi.astype(BF16).astype(F32), 0.0)
    feats = phi.shape[1]
    state, end = payload(
        dot_tn(tail.astype(BF16), vx_out[WIN : WIN + length, :]),
        jnp.sum(tail, axis=0, keepdims=True),
        last_id,
    )
    sbuf[0:feats, :] = state
    sbuf[feats : feats + TAIL, :] = end
    for k in range(REACH):
        copy = remote(sbuf, rbuf.at[k], xs.at[k], xr.at[k], context=lax.rem(here + k + 1, count))
        copy.start()
        sends.append(copy)
    for k in range(REACH):
        whole(rbuf.at[k], xr.at[k]).wait()
    state_in, norm_in = gathered(rbuf, first_id, here, count, True)
    state_out[...] = state_in.astype(BF16)
    norm_out[...] = jnp.broadcast_to(norm_in, norm_out.shape)
    for copy in rims:
        copy.wait()
    rim_out[...] = jnp.where(here > 0, rim_in[...], -1)
    whole(q_out, qr).wait()
    for copy in sends:
        copy.wait_send()


def core_kernel(
    q_ref, kx_ref, vx_ref, rim_ref, seg_ref, fq_ref, phik_ref, state_ref, norm_ref,
    err_ref, gq_ref, dphik_ref, cot_ref,
    mask, bias, take, phi_s, slope_s, dn_s, dd_s, acc,
):
    heads, width, feats = fq_ref.shape
    length = q_ref.shape[0]
    step = 256
    inv_scale = 1.0 / math.sqrt(width)

    seg_row = seg_ref[...]
    first_id = jnp.min(seg_row, axis=1, keepdims=True).astype(F32)
    rows_f = seg_row.astype(F32)
    rim_f = rim_ref[...].astype(F32)
    seg_col = columns_of(seg_row)
    take[...] = jnp.where(seg_col == first_id, 1.0, 0.0)
    r = lax.broadcasted_iota(jnp.int32, (128, 128), 0)
    c = lax.broadcasted_iota(jnp.int32, (128, 128), 1)
    for i in range(0, length, 128):
        col = seg_col[i : i + 128, :]
        for j in range(0, length, 128):
            if j > i:
                mask[i : i + 128, j : j + 128] = jnp.zeros((128, 128), F32)
                continue
            same = col == rows_f[:, j : j + 128]
            if j == i:
                same = same & (c <= r)
            mask[i : i + 128, j : j + 128] = jnp.where(same, 1.0, 0.0)
        before = rim_f if i == 0 else rows_f[:, i - 128 : i]
        bias[i : i + 128, 0:128] = jnp.where((col == before) & (c > r), 0.0, -1e30)
        bias[i : i + 128, 128:256] = jnp.where(
            (col == rows_f[:, i : i + 128]) & (c <= r), 0.0, -1e30
        )

    def lanes(h):
        return pl.ds(pl.multiple_of(h * width, 128), width)

    cot_ref[...] = jnp.zeros_like(cot_ref)
    acc[...] = jnp.zeros_like(acc)
    dphik_ref[...] = jnp.zeros_like(dphik_ref)

    def forward(h, _):
        q = q_ref[:, lanes(h)]
        pre = dot_nn(q, fq_ref[h])
        small = jnp.exp(jnp.minimum(pre, 0.0))
        phi = jnp.where(pre > 0, pre + 1.0, small).astype(BF16)
        slope_s[h] = jnp.where(pre > 0, 1.0, small)
        phi_s[h] = phi
        norm = norm_ref[0:1, :]
        dns, dds = [], []
        for i in range(0, length, step):
            end = i + step
            part = phi[i:end]
            score = dot_nt(part, phik_ref[0:end, :]) * mask[i:end, 0:end]
            own = take[i:end, :]
            numer = dot_nn(score.astype(BF16), vx_ref[WIN : WIN + end, :])
            numer += own * dot_nn(part, state_ref[...])
            denom = jnp.sum(score, axis=1, keepdims=True)
            denom += jnp.sum(own * (part.astype(F32) * norm), axis=1, keepdims=True)
            inv = 1.0 / denom
            student = numer * inv
            teachers = []
            for j in range(i, end, 128):
                logits = dot_nt(q[j : j + 128], kx_ref[j : j + 256, :]) * inv_scale
                logits += bias[j : j + 128, :]
                probs = jnp.exp(logits - jnp.max(logits, axis=1, keepdims=True))
                total = jnp.sum(probs, axis=1, keepdims=True)
                teachers.append(dot_nn(probs.astype(BF16), vx_ref[j : j + 256, :]) / total)
            gap = student - jnp.concatenate(teachers, axis=0)
            err_ref[i:end, lanes(h)] = gap.astype(BF16)
            up = 32.0 * gap
            dn = (up * inv).astype(BF16)
            dd = -jnp.sum(up * student, axis=1, keepdims=True) * inv
            dn_s[h, i:end, :] = dn
            dd_s[h, i:end, :] = dd
            dns.append(dn)
            dds.append(dd)
        lead = phi.astype(F32) * take[...]
        acc[...] += jnp.sum(
            (lead * jnp.concatenate(dds, axis=0)).reshape(length // 8, 8, feats), axis=0
        )
        cot_ref[0:feats, :] += dot_tn(lead.astype(BF16), jnp.concatenate(dns, axis=0))
        return 0

    lax.fori_loop(0, heads, forward, 0)
    last_id = jnp.max(seg_row, axis=1, keepdims=True)
    row = lax.broadcasted_iota(jnp.int32, (TAIL, feats), 0)
    total = jnp.sum(acc[...], axis=0, keepdims=True)
    cot_ref[feats : feats + TAIL, :] = jnp.where(
        row == 0, total, jnp.where(row == 1, first_id, 0.0)
    )

    def backward(h, _):
        q = q_ref[:, lanes(h)]
        norm = norm_ref[0:1, :]
        outs = []
        for i in range(0, length, step):
            end = i + step
            dn = dn_s[h, i:end, :]
            dd = dd_s[h, i:end, :]
            own = take[i:end, :]
            d_score = dot_nt(dn, vx_ref[WIN : WIN + end, :]) + dd
            d_score = (d_score * mask[i:end, 0:end]).astype(BF16)
            d_phi = dot_nn(d_score, phik_ref[0:end, :])
            d_phi += own * (dot_nt(dn, state_ref[...]) + dd * norm)
            dphik_ref[0:end, :] += dot_tn(d_score, phi_s[h, i:end, :])
            outs.append((d_phi * slope_s[h, i:end, :]).astype(BF16))
        gq_ref[h] = dot_tn(q, jnp.concatenate(outs, axis=0)).astype(BF16)
        return 0

    lax.fori_loop(0, heads, backward, 0)
    del last_id


def leave_kernel(
    gq_ref, cot_ref, dphik_ref, slope_ref, kx_ref, vx_ref, fk_ref, seg_ref,
    gq_out, keys_out, gk_out,
    sbuf, rbuf, part, red, spread, kpart, kparts, kred, kspread,
    xs, xr, s1, r1, s2, r2, s3, r3, s4, r4,
):
    here = lax.axis_index("context")
    count = lax.axis_size("context")
    feats, width = cot_ref.shape[0] - TAIL, cot_ref.shape[1]
    length = dphik_ref.shape[0]
    scale = 1.0 / math.sqrt(length * count)

    barrier = pltpu.get_barrier_semaphore()

    def greet(k, _):
        pl.semaphore_signal(
            barrier, inc=1, device_id={"context": lax.rem(here + k, count)}, device_id_type=MESH
        )
        return 0

    lax.fori_loop(1, count, greet, 0)
    sbuf[...] = cot_ref[...].astype(BF16)
    pl.semaphore_wait(barrier, count - 1)

    sends = []
    for k in range(REACH):
        copy = remote(
            sbuf, rbuf.at[k], xs.at[k], xr.at[k], context=lax.rem(here + count - k - 1, count)
        )
        copy.start()
        sends.append(copy)

    pltpu.make_async_copy(gq_ref.at[here], part.at[here], r1).start()

    def scatter(k, _):
        peer = lax.rem(here + k, count)
        remote(gq_ref.at[peer], part.at[here], s1, r1, context=peer).start()
        return 0

    lax.fori_loop(1, count, scatter, 0)

    for k in range(REACH):
        whole(rbuf.at[k], xr.at[k]).wait()
    seg_row = seg_ref[...]
    last_id = jnp.max(seg_row, axis=1, keepdims=True).astype(F32)
    back, back_norm = gathered(rbuf, last_id, here, count, False)
    own = jnp.where(columns_of(seg_row) == last_id, 1.0, 0.0)
    d_phi = dphik_ref[...] + own * (
        dot_nt(vx_ref[WIN : WIN + length, :], back.astype(BF16)) + back_norm
    )
    d_pre = (d_phi * slope_ref[...]).astype(BF16)
    keys_out[...] = dot_nt(d_pre, fk_ref[...]).astype(BF16)
    grad = dot_tn(kx_ref[WIN : WIN + length, :], d_pre)
    share = kpart.shape[0]
    kpart[...] = grad.reshape(share, width // share, feats)

    pltpu.make_async_copy(kpart.at[here // 2], kparts.at[here], r3).start()

    def scatter_k(k, _):
        peer = lax.rem(here + k, count)
        remote(kpart.at[peer // 2], kparts.at[here], s3, r3, context=peer).start()
        return 0

    lax.fori_loop(1, count, scatter_k, 0)

    whole(part, r1).wait()
    red[...] = jnp.sum(part[...].astype(F32), axis=0).astype(BF16)
    pltpu.make_async_copy(red, spread.at[here], r2).start()

    def spread_q(k, _):
        peer = lax.rem(here + k, count)
        remote(red, spread.at[here], s2, r2, context=peer).start()
        return 0

    lax.fori_loop(1, count, spread_q, 0)

    whole(kparts, r3).wait()
    kred[...] = jnp.sum(kparts[...], axis=0)
    pltpu.make_async_copy(kred, kspread.at[here // 2], r4).start()

    def spread_k(k, _):
        peer = lax.rem(here + 2 * k, count)
        remote(kred, kspread.at[here // 2], s4, r4, context=peer).start()
        return 0

    lax.fori_loop(1, count // 2, spread_k, 0)

    whole(spread, r2).wait()
    gq_out[...] = spread[...].astype(F32) * scale
    whole(kspread, r4).wait()
    gk_out[...] = kspread[...] * scale

    for copy in sends:
        copy.wait_send()
    rest = pl.ds(0, count - 1)
    whole(part.at[rest], s1).wait()
    whole(spread.at[rest], s2).wait()
    whole(kparts.at[rest], s3).wait()
    whole(kspread.at[pl.ds(0, count // 2 - 1)], s4).wait()


def on_device(queries, keys, values, segments, feat_q, feat_k):
    rows = keys.shape[0]
    split = lax.axis_size("ulysses")
    count = lax.axis_size("context")
    heads, width, feats = feat_q.shape
    length = rows * split
    seg = segments.reshape(1, length)
    key_map = feat_k.reshape(width, feats)
    shape = jax.ShapeDtypeStruct
    anyway = pl.BlockSpec(memory_space=pl.ANY)
    vmem = pl.BlockSpec(memory_space=pltpu.VMEM)
    dma = pltpu.SemaphoreType.DMA
    ext = length + WIN

    q_all, kx, vx, rim, phi_k, slope_k, state, norm = pl.pallas_call(
        enter_kernel,
        name="enter",
        out_shape=(
            shape((length, heads * width), BF16),
            shape((ext, width), BF16),
            shape((ext, width), BF16),
            shape((1, WIN), jnp.int32),
            shape((length, feats), BF16),
            shape((length, feats), F32),
            shape((feats, width), BF16),
            shape((8, feats), F32),
        ),
        in_specs=[anyway, anyway, anyway, vmem, vmem],
        out_specs=[vmem] * 8,
        scratch_shapes=[
            pltpu.VMEM((feats + TAIL, width), BF16),
            pltpu.VMEM((REACH, feats + TAIL, width), BF16),
            pltpu.VMEM((1, WIN), jnp.int32),
            dma((split - 1,)),
            dma((split - 1,)),
            dma((split - 1,)),
            dma,
            dma,
            dma,
            dma((3,)),
            dma((3,)),
            dma((REACH,)),
            dma((REACH,)),
        ],
        compiler_params=pltpu.CompilerParams(collective_id=0, has_side_effects=True),
    )(queries, keys, values, seg, key_map)

    errors, grad_q, d_phi_k, cot = pl.pallas_call(
        core_kernel,
        name="core",
        out_shape=(
            shape((length, heads * width), BF16),
            shape((heads, width, feats), BF16),
            shape((length, feats), F32),
            shape((feats + TAIL, width), F32),
        ),
        in_specs=[vmem] * 9,
        out_specs=[vmem] * 4,
        scratch_shapes=[
            pltpu.VMEM((length, length), F32),
            pltpu.VMEM((length, 2 * WIN), F32),
            pltpu.VMEM((length, 128), F32),
            pltpu.VMEM((heads, length, feats), BF16),
            pltpu.VMEM((heads, length, feats), F32),
            pltpu.VMEM((heads, length, width), BF16),
            pltpu.VMEM((heads, length, 1), F32),
            pltpu.VMEM((8, feats), F32),
        ],
    )(q_all, kx, vx, rim, seg, feat_q, phi_k, state, norm)

    per = heads * width // count
    share = count // 2
    grad_q, grad_keys, grad_k = pl.pallas_call(
        leave_kernel,
        name="leave",
        out_shape=(
            shape((count, per, feats), F32),
            shape((length, width), BF16),
            shape((share, width // share, feats), F32),
        ),
        in_specs=[vmem] * 8,
        out_specs=[vmem] * 3,
        scratch_shapes=[
            pltpu.VMEM((feats + TAIL, width), BF16),
            pltpu.VMEM((REACH, feats + TAIL, width), BF16),
            pltpu.VMEM((count, per, feats), BF16),
            pltpu.VMEM((per, feats), BF16),
            pltpu.VMEM((count, per, feats), BF16),
            pltpu.VMEM((share, width // share, feats), F32),
            pltpu.VMEM((count, width // share, feats), F32),
            pltpu.VMEM((width // share, feats), F32),
            pltpu.VMEM((share, width // share, feats), F32),
            dma((REACH,)),
            dma((REACH,)),
        ]
        + [dma] * 8,
        compiler_params=pltpu.CompilerParams(collective_id=1, has_side_effects=True),
    )(grad_q.reshape(count, per, feats), cot, d_phi_k, slope_k, kx, vx, key_map, seg)
    return (
        errors,
        grad_keys,
        grad_q.reshape(heads, width, feats),
        grad_k.reshape(feat_k.shape),
    )


def solution(mesh):
    in_specs = (
        P(("dp", "context", "ulysses"), None),
        P(("dp", "context", "ulysses"), None),
        P(("dp", "context", "ulysses"), None),
        P(("dp", "context")),
        P("ulysses", None, None),
        P("ulysses", None, None),
    )
    out_specs = (
        P(("dp", "context"), "ulysses"),
        P(("dp", "context"), "ulysses"),
        P(("dp", "ulysses"), None, None),
        P(("dp", "ulysses"), None, None),
    )
    return jax.shard_map(
        on_device, mesh=mesh, in_specs=in_specs, out_specs=out_specs, check_vma=False
    )
```

time: 727 us -> 91.5 us (0.13); the launches traced: 718 us -> 91.3 us
  blocking collectives: 232 us -> 0 us
  waiting for transfers between devices: 183 us -> 0 us
  loops' own time: 123 us -> 0 us
  Pallas kernels: 0 us -> 86.5 us
  local copies, waits for them, and re-layouts: 61.8 us -> 4.1 us
  matrix products: 44.6 us -> 0 us
  other arithmetic: 35.4 us -> 0 us
  starting transfers between devices: 23.5 us -> 0 us
  between operations: 14.2 us -> 0.65 us
    psum x1 -> x0, blocking collectives: 136 us -> none  [on_device(): lax.psum(grad_key_maps.astype(jnp.bfloat16), 'context').astype(jnp.float32)]
    another operation x2 -> x0, loops' own time: 123 us -> none  [entering(): return lax.fori_loop(0, count - 1, lap, so_far)]
    psum x1 -> x0, waiting for transfers between devices: 102 us -> none  [on_device(): lax.psum(grad_query_maps.astype(jnp.bfloat16), 'context')]
    pallas_call x0 -> x3, Pallas kernels: none -> 86.5 us  [the longest x1 38.7 us: on_device(): pl.pallas_call(leave_kernel, name='leave', out_shape=(shape((count, per,...]
    all_gather x2 -> x0, waiting for transfers between devices: 76.1 us -> none  [entering(): pieces = jax.tree.map(lambda part: lax.all_gather(part, axis), value)]
    all_gather x2 -> x0, blocking collectives: 74 us -> none  [entering(): pieces = jax.tree.map(lambda part: lax.all_gather(part, axis), value)]
    dot_general x21 -> x0, matrix products: 44.6 us -> none  [widened(): return jnp.einsum(form, left, right, preferred_element_type=jnp.float32)]
    dynamic_slice x62 -> x0, local copies, waits for them, and re-layouts: 36.4 us -> none  [lap(): longer = join(so_far, jax.tree.map(lambda part: part[position], pieces))]
  transfers between devices with their start and end apart: 9 -> 0, of which waited for: 3 -> 0; matrix products, arithmetic and copies ran while one was open for 12% -> 0% of each run, Pallas kernels for 0% -> 0%
where the time goes in v1:
time: 91.5 us; the launch traced here: 91.3 us
  Pallas kernels  86.5 us (95%)
  local copies, waits for them, and re-layouts  4.1 us (4%)
    pallas_call x1, Pallas kernels, on_device(): pl.pallas_call(leave_kernel, name='leave', out_shape=(shape((count, per,...  38.7 us
    pallas_call x1, Pallas kernels, on_device(): pl.pallas_call(enter_kernel, name='enter', out_shape=(shape((length, head...  28.2 us
    pallas_call x1, Pallas kernels, on_device(): pl.pallas_call(core_kernel, name='core', out_shape=(shape((length, heads...  19.7 us
    unnamed x5, local copies, waits for them, and re-layouts  4.1 us

profile of v1, /device:TPU:2, one launch (start us, length us, event | category | flops | bytes accessed | tf_op | source)
XLA Modules:
  0.0 91.3 jit_solution(14827949586028172000)
XLA Ops:
  0.6 28.2 %enter.1 = (bf16[512,1024]{1,0:T(8,128)(2,1)}, bf16[640,128]{1,0:T(8,128)(2,1)}, bf16[640,128]{1,0:T(8,128)(2,1)}, s32[1,128]{1,0:T(1,128)}, bf16[512,128]{1,0:T...) custom-call(bf16[128,4096]{1,0:T(8,128)(2,1)} %q_ref.1, bf16[128,512]{1,0:T(8,128)(2,1)} %k_ref.1, ...), custom_call_target="tpu_custom_call" | custom-call | tf_op jit(solution)/shard_map/enter/pallas_call | solution.py:390
  28.8 19.7 %core.1 = (bf16[512,1024]{1,0:T(8,128)(2,1)}, bf16[8,128,128]{2,1,0:T(8,128)(2,1)}, f32[512,128]{1,0:T(8,128)}, f32[144,128]{1,0:T(8,128)}) custom-call(bf16[512,1024]{1,0:T(8,128)(2,1)} %get-tuple-element.19.q_ref, bf16[640,128]{1,0:T(8,128)(2,1)} %get-tuple-element.20.kx_ref, bf16[640,128]{1,0:T(8,128)(2,1)} %get-tuple-element.21.vx_ref, ...), custom_call_target="tpu_custom_call" | custom-call | tf_op jit(solution)/shard_map/core/pallas_call | solution.py:423
  48.5 38.7 %leave.1 = (f32[32,32,128]{2,1,0:T(8,128)}, bf16[512,128]{1,0:T(8,128)(2,1)}, f32[16,8,128]{2,1,0:T(8,128)}) custom-call(bf16[32,32,128]{2,1,0:T(8,128)(2,1)} %bitcast.6, f32[144,128]{1,0:T(8,128)} %get-tuple-element.28.cot_ref, f32[512,128]{1,0:T(8,128)} %get-tuple-element.29.dphik_ref, f32[512,128]{1,0:T(8,128)} %get-tuple-element.30.slope_ref, ...), custom_call_target="tpu_custom_call" | custom-call | tf_op jit(solution)/shard_map/leave/pallas_call | solution.py:448
  87.1 1.6 %copy.13 = bf16[512,128]{1,0:T(8,128)(2,1)} copy(bf16[512,128]{1,0:T(8,128)(2,1)} %get-tuple-element.39) | data formatting | bytes 262144
  88.7 0.0 copy-start
  88.7 1.9 %copy.14 = f32[8,128,128]{2,1,0:T(8,128)} copy(f32[8,128,128]{2,1,0:T(8,128)} %bitcast.5) | data formatting | bytes 1048576
  90.6 0.0 copy-done
  90.6 0.6 copy.15
Async XLA Ops:
  88.7 1.9 %copy-start = (f32[16,8,128]{2,1,0:T(8,128)S(1)}, f32[16,8,128]{2,1,0:T(8,128)}, u32[]{:S(2)}) copy-start(f32[16,8,128]{2,1,0:T(8,128)} %get-tuple-element.33) | copy-start | bytes 196612

commit v2 on v1

v2 whole, which is shorter than its diff:
```python
import functools
import math

import jax
import jax.numpy as jnp
from jax import lax
from jax.experimental import pallas as pl
from jax.experimental.pallas import tpu as pltpu
from jax.sharding import PartitionSpec as P

WIN = 128
REACH = 8
TAIL = 16
MESH = pl.DeviceIdType.MESH
F32 = jnp.float32
BF16 = jnp.bfloat16


def dot_nn(a, b):
    return lax.dot_general(a, b, (((1,), (0,)), ((), ())), preferred_element_type=F32)


def dot_nt(a, b):
    return lax.dot_general(a, b, (((1,), (1,)), ((), ())), preferred_element_type=F32)


def dot_tn(a, b):
    return lax.dot_general(a, b, (((0,), (0,)), ((), ())), preferred_element_type=F32)


def remote(src, dst, send, recv, **where):
    return pltpu.make_async_remote_copy(
        src_ref=src, dst_ref=dst, send_sem=send, recv_sem=recv, device_id=where, device_id_type=MESH
    )


def whole(ref, sem):
    return pltpu.make_async_copy(ref, ref, sem)


def columns_of(seg_row):
    length = seg_row.shape[1]
    parts = [
        jnp.transpose(jnp.broadcast_to(seg_row[:, i : i + 128].astype(F32), (128, 128)))
        for i in range(0, length, 128)
    ]
    return jnp.concatenate(parts, axis=0)


def payload(state, norm, ident):
    row = lax.broadcasted_iota(jnp.int32, (TAIL, norm.shape[1]), 0)
    tail = jnp.where(row == 0, norm, jnp.where(row == 1, ident, 0.0))
    return state.astype(BF16), tail.astype(BF16)


def gathered(buf, ident, here, count, forward):
    feats = buf.shape[1] - TAIL
    state = jnp.zeros((feats, buf.shape[2]), F32)
    norm = jnp.zeros((1, buf.shape[2]), F32)
    for k in range(REACH):
        inside = here > k if forward else here + k + 1 < count
        tail = buf[k, feats : feats + TAIL, :].astype(F32)
        keep = (tail[1:2, :] == ident) & inside
        state += jnp.where(keep, buf[k, 0:feats, :].astype(F32), 0.0)
        norm += jnp.where(keep, tail[0:1, :], 0.0)
    return state, norm


def step_kernel(
    q_ref, k_ref, v_ref, seg_in, fq_ref, fk_ref,
    err_ref, keys_out, spread, kspread,
    seg_ref, qv, qb, kx, vx, fq, fk, rim_in, sbuf, rbuf, cbuf, dbuf,
    mask, bias, take, lead_s, phi_s, slope_s, num_s, den_s, tea_s, dn_s, dd_s, phik, slopek, dphik, cot, acc,
    gq, part, red, kpart, kparts, kred,
    ql, kl, vl, fl, ks, vs, qs, kr, vr, qr, rs, rr, xs, xr, cs, cr,
    s1, r1, s2, r2, s3, r3, s4, r4,
):
    here, mine = lax.axis_index("context"), lax.axis_index("ulysses")
    count, split = lax.axis_size("context"), lax.axis_size("ulysses")
    rows = k_ref.shape[0]
    heads, width, feats = fq_ref.shape
    length = rows * split
    wide = heads * width
    step = 256
    inv_scale = 1.0 / math.sqrt(width)

    barrier = pltpu.get_barrier_semaphore()
    for j in range(1, split):
        pl.semaphore_signal(
            barrier, inc=1, device_id={"ulysses": lax.rem(mine + j, split)}, device_id_type=MESH
        )

    def greet(k, _):
        pl.semaphore_signal(
            barrier, inc=1, device_id={"context": lax.rem(here + k, count)}, device_id_type=MESH
        )
        return 0

    lax.fori_loop(1, count, greet, 0)

    def place(start):
        return pl.ds(pl.multiple_of(start + mine * rows, 128), rows)

    def lanes(who, size):
        return pl.ds(pl.multiple_of(who * size, 128), size)

    load_seg = pltpu.make_async_copy(seg_in, seg_ref, fl.at[2])
    load_seg.start()
    small = ((k_ref, kx, kl, ks, kr), (v_ref, vx, vl, vs, vr))
    for src, dst, _, _, recv in small:
        pltpu.make_async_copy(src.at[:, lanes(mine, width)], dst.at[place(WIN), :], recv).start()
    load_q = pltpu.make_async_copy(q_ref, qv, ql)
    load_q.start()
    loads = [pltpu.make_async_copy(fq_ref, fq, fl.at[0]), pltpu.make_async_copy(fk_ref, fk, fl.at[1])]
    for copy in loads:
        copy.start()

    load_seg.wait()
    seg_row = seg_ref[...]
    rows_f = seg_row.astype(F32)
    first_id = jnp.min(seg_row, axis=1, keepdims=True).astype(F32)
    last_id = jnp.max(seg_row, axis=1, keepdims=True).astype(F32)
    seg_col = columns_of(seg_row)
    take[...] = jnp.where(seg_col == first_id, 1.0, 0.0)
    r = lax.broadcasted_iota(jnp.int32, (128, 128), 0)
    c = lax.broadcasted_iota(jnp.int32, (128, 128), 1)
    for i in range(0, length, 128):
        col = seg_col[i : i + 128, :]
        for j in range(0, length, 128):
            if j > i:
                mask[i : i + 128, j : j + 128] = jnp.zeros((128, 128), F32)
                continue
            same = col == rows_f[:, j : j + 128]
            if j == i:
                same = same & (c <= r)
            mask[i : i + 128, j : j + 128] = jnp.where(same, 1.0, 0.0)
        if i:
            bias[i : i + 128, 0:128] = jnp.where(
                (col == rows_f[:, i - 128 : i]) & (c > r), 0.0, -1e30
            )
        bias[i : i + 128, 128:256] = jnp.where(
            (col == rows_f[:, i : i + 128]) & (c <= r), 0.0, -1e30
        )
    cot[...] = jnp.zeros_like(cot)
    acc[...] = jnp.zeros_like(acc)
    dphik[...] = jnp.zeros_like(dphik)
    load_q.wait()
    for h in range(heads):
        pltpu.make_async_copy(
            qv.at[:, lanes(mine * heads + h, width)], qb.at[h, place(0), :], qr.at[h]
        ).start()

    pl.semaphore_wait(barrier, split - 1 + count - 1)

    sends = []
    for src, dst, _, send, recv in small:
        for j in range(1, split):
            peer = lax.rem(mine + j, split)
            copy = remote(
                src.at[:, lanes(peer, width)], dst.at[place(WIN), :], send.at[j - 1], recv, ulysses=peer
            )
            copy.start()
            sends.append(copy)

    def send_q(h, _):
        for j in range(1, split):
            peer = lax.rem(mine + j, split)
            remote(
                qv.at[:, lanes(peer * heads + h, width)], qb.at[h, place(0), :], qs, qr.at[h],
                ulysses=peer,
            ).start()
        return 0

    lax.fori_loop(0, heads, send_q, 0)

    for copy in loads:
        copy.wait()
    whole(kx.at[pl.ds(WIN, length), :], kr).wait()
    whole(vx.at[pl.ds(WIN, length), :], vr).wait()
    after = lax.rem(here + 1, count)
    edge, rim = pl.ds(length, WIN), pl.ds(0, WIN)
    rims = [
        remote(kx.at[edge, :], kx.at[rim, :], rs.at[0], rr.at[0], context=after),
        remote(vx.at[edge, :], vx.at[rim, :], rs.at[1], rr.at[1], context=after),
        remote(seg_ref.at[:, pl.ds(length - WIN, WIN)], rim_in, rs.at[2], rr.at[2], context=after),
    ]
    for copy in rims:
        copy.start()

    pre = dot_nn(kx[WIN : WIN + length, :], fk[...])
    low = jnp.exp(jnp.minimum(pre, 0.0))
    phi = jnp.where(pre > 0, pre + 1.0, low).astype(BF16)
    phik[...] = phi
    slopek[...] = jnp.where(pre > 0, 1.0, low)
    tail = jnp.where(seg_col == last_id, phi.astype(F32), 0.0)
    state, end = payload(
        dot_tn(tail.astype(BF16), vx[WIN : WIN + length, :]),
        jnp.sum(tail, axis=0, keepdims=True),
        last_id,
    )
    sbuf[0:feats, :] = state
    sbuf[feats : feats + TAIL, :] = end
    for k in range(REACH):
        copy = remote(sbuf, rbuf.at[k], xs.at[k], xr.at[k], context=lax.rem(here + k + 1, count))
        copy.start()
        sends.append(copy)

    for copy in rims:
        copy.wait()
    rim_f = jnp.where(here > 0, rim_in[...], -1).astype(F32)
    bias[0:128, 0:128] = jnp.where((seg_col[0:128, :] == rim_f) & (c > r), 0.0, -1e30)

    def forward(h, _):
        whole(qb.at[h], qr.at[h]).wait()
        q = qb[h]
        pre = dot_nn(q, fq[h])
        low = jnp.exp(jnp.minimum(pre, 0.0))
        phi = jnp.where(pre > 0, pre + 1.0, low).astype(BF16)
        slope_s[h] = jnp.where(pre > 0, 1.0, low)
        phi_s[h] = phi
        lead_s[h] = (phi.astype(F32) * take[...]).astype(BF16)
        for i in range(0, length, step):
            end = i + step
            score = dot_nt(phi[i:end], phik[0:end, :]) * mask[i:end, 0:end]
            num_s[h, i:end, :] = dot_nn(score.astype(BF16), vx[WIN : WIN + end, :])
            den_s[h, i:end, :] = jnp.sum(score, axis=1, keepdims=True)
            for j in range(i, end, 128):
                logits = dot_nt(q[j : j + 128], kx[j : j + 256, :]) * inv_scale
                logits += bias[j : j + 128, :]
                probs = jnp.exp(logits - jnp.max(logits, axis=1, keepdims=True))
                total = jnp.sum(probs, axis=1, keepdims=True)
                tea_s[h, j : j + 128, :] = dot_nn(probs.astype(BF16), vx[j : j + 256, :]) / total
        return 0

    lax.fori_loop(0, heads, forward, 0)

    for k in range(REACH):
        whole(rbuf.at[k], xr.at[k]).wait()
    state, norm = gathered(rbuf, first_id, here, count, True)
    state = state.astype(BF16)

    def meet(h, _):
        lead = lead_s[h]
        lead_f = lead.astype(F32)
        numer = num_s[h] + dot_nn(lead, state)
        denom = den_s[h] + jnp.sum(lead_f * norm, axis=1, keepdims=True)
        inv = 1.0 / denom
        student = numer * inv
        gap = student - tea_s[h]
        err_ref[:, lanes(h, width)] = gap.astype(BF16)
        up = 32.0 * gap
        dn = (up * inv).astype(BF16)
        dd = -jnp.sum(up * student, axis=1, keepdims=True) * inv
        dn_s[h] = dn
        dd_s[h] = dd
        acc[...] += jnp.sum((lead_f * dd).reshape(length // 8, 8, feats), axis=0)
        cot[...] += dot_tn(lead, dn)
        return 0

    lax.fori_loop(0, heads, meet, 0)
    total, end = payload(cot[...], jnp.sum(acc[...], axis=0, keepdims=True), first_id)
    cbuf[0:feats, :] = total
    cbuf[feats : feats + TAIL, :] = end
    for k in range(REACH):
        copy = remote(
            cbuf, dbuf.at[k], cs.at[k], cr.at[k], context=lax.rem(here + count - k - 1, count)
        )
        copy.start()
        sends.append(copy)

    per = gq.shape[1]
    share = width // per

    def head_of(s):
        return lax.rem(s + here // share, heads)

    def scatter(s):
        for j in range(share):
            owner = head_of(s) * share + j

            @pl.when(owner != here)
            def _():
                remote(gq.at[owner], part.at[here], s1, r1, context=owner).start()

            @pl.when(owner == here)
            def _():
                pltpu.make_async_copy(gq.at[owner], part.at[here], r1).start()

    def backward(s, _):
        h = head_of(s)

        @pl.when(s > 0)
        def _():
            scatter(s - 1)

        outs = []
        for i in range(0, length, step):
            end = i + step
            dn = dn_s[h, i:end, :]
            dd = dd_s[h, i:end, :]
            d_score = dot_nt(dn, vx[WIN : WIN + end, :]) + dd
            d_score = (d_score * mask[i:end, 0:end]).astype(BF16)
            d_phi = dot_nn(d_score, phik[0:end, :])
            d_phi += take[i:end, :] * (dot_nt(dn, state) + dd * norm)
            dphik[0:end, :] += dot_tn(d_score, phi_s[h, i:end, :])
            outs.append((d_phi * slope_s[h, i:end, :]).astype(BF16))
        grad = dot_tn(qb[h], jnp.concatenate(outs, axis=0)).astype(BF16)
        for j in range(share):
            gq[h * share + j] = grad[j * per : (j + 1) * per, :]
        return 0

    lax.fori_loop(0, heads, backward, 0)
    scatter(heads - 1)

    for k in range(REACH):
        whole(dbuf.at[k], cr.at[k]).wait()
    back, back_norm = gathered(dbuf, last_id, here, count, False)
    own = jnp.where(columns_of(seg_ref[...]) == last_id, 1.0, 0.0)
    d_phi = dphik[...] + own * (dot_nt(vx[WIN : WIN + length, :], back.astype(BF16)) + back_norm)
    d_pre = (d_phi * slopek[...]).astype(BF16)
    grad = dot_tn(kx[WIN : WIN + length, :], d_pre)
    kpart[...] = grad.reshape(kpart.shape)

    pltpu.make_async_copy(kpart.at[here // 2], kparts.at[here], r3).start()

    def scatter_k(k, _):
        peer = lax.rem(here + k, count)
        remote(kpart.at[peer // 2], kparts.at[here], s3, r3, context=peer).start()
        return 0

    lax.fori_loop(1, count, scatter_k, 0)
    keys_out[...] = dot_nt(d_pre, fk[...]).astype(BF16)

    whole(part, r1).wait()
    red[...] = jnp.sum(part[...].astype(F32), axis=0).astype(BF16)
    pltpu.make_async_copy(red, spread.at[here], r2).start()

    def spread_q(k, _):
        peer = lax.rem(here + k, count)
        remote(red, spread.at[here], s2, r2, context=peer).start()
        return 0

    lax.fori_loop(1, count, spread_q, 0)

    whole(kparts, r3).wait()
    kred[...] = jnp.sum(kparts[...], axis=0)
    pltpu.make_async_copy(kred, kspread.at[here // 2], r4).start()

    def spread_k(k, _):
        peer = lax.rem(here + 2 * k, count)
        remote(kred, kspread.at[here // 2], s4, r4, context=peer).start()
        return 0

    lax.fori_loop(1, count // 2, spread_k, 0)

    for copy in sends:
        copy.wait_send()
    whole(qb.at[:, pl.ds(0, length - rows), :], qs).wait()
    rest = pl.ds(0, count - 1)
    whole(part.at[rest], s1).wait()
    whole(kparts.at[rest], s3).wait()
    whole(spread.at[rest], s2).wait()
    whole(kspread.at[pl.ds(0, count // 2 - 1)], s4).wait()
    whole(spread, r2).wait()
    whole(kspread, r4).wait()


def store_kernel(scale, err_in, keys_in, gq_in, gk_in, err_out, keys_out, gq_out, gk_out):
    err_out[...] = err_in[...]
    keys_out[...] = keys_in[...]
    gq_out[...] = gq_in[...].astype(F32) * scale
    gk_out[...] = gk_in[...] * scale


def on_device(queries, keys, values, segments, feat_q, feat_k):
    rows = keys.shape[0]
    split = lax.axis_size("ulysses")
    count = lax.axis_size("context")
    heads, width, feats = feat_q.shape
    length = rows * split
    seg = segments.reshape(1, length)
    key_map = feat_k.reshape(width, feats)
    per = heads * width // count
    share = count // 2
    shape = jax.ShapeDtypeStruct
    hbm = pl.BlockSpec(memory_space=pltpu.HBM)
    vmem = pl.BlockSpec(memory_space=pltpu.VMEM)
    dma = pltpu.SemaphoreType.DMA
    stay = functools.partial(pltpu.with_memory_space_constraint, memory_space=pltpu.HBM)
    ext = length + WIN
    packed = feats + TAIL

    outs = pl.pallas_call(
        step_kernel,
        name="step",
        out_shape=(
            shape((length, heads * width), BF16),
            shape((length, width), BF16),
            shape((count, per, feats), BF16),
            shape((share, width // share, feats), F32),
        ),
        in_specs=[hbm] * 6,
        out_specs=[vmem] * 4,
        scratch_shapes=[
            pltpu.VMEM((1, length), jnp.int32),
            pltpu.VMEM((rows, queries.shape[1]), BF16),
            pltpu.VMEM((heads, length, width), BF16),
            pltpu.VMEM((ext, width), BF16),
            pltpu.VMEM((ext, width), BF16),
            pltpu.VMEM((heads, width, feats), BF16),
            pltpu.VMEM((width, feats), BF16),
            pltpu.VMEM((1, WIN), jnp.int32),
            pltpu.VMEM((packed, width), BF16),
            pltpu.VMEM((REACH, packed, width), BF16),
            pltpu.VMEM((packed, width), BF16),
            pltpu.VMEM((REACH, packed, width), BF16),
            pltpu.VMEM((length, length), F32),
            pltpu.VMEM((length, 2 * WIN), F32),
            pltpu.VMEM((length, feats), F32),
            pltpu.VMEM((heads, length, feats), BF16),
            pltpu.VMEM((heads, length, feats), BF16),
            pltpu.VMEM((heads, length, feats), F32),
            pltpu.VMEM((heads, length, width), F32),
            pltpu.VMEM((heads, length, 1), F32),
            pltpu.VMEM((heads, length, width), F32),
            pltpu.VMEM((heads, length, width), BF16),
            pltpu.VMEM((heads, length, 1), F32),
            pltpu.VMEM((length, feats), BF16),
            pltpu.VMEM((length, feats), F32),
            pltpu.VMEM((length, feats), F32),
            pltpu.VMEM((feats, width), F32),
            pltpu.VMEM((8, feats), F32),
            pltpu.VMEM((count, per, feats), BF16),
            pltpu.VMEM((count, per, feats), BF16),
            pltpu.VMEM((per, feats), BF16),
            pltpu.VMEM((share, width // share, feats), F32),
            pltpu.VMEM((count, width // share, feats), F32),
            pltpu.VMEM((width // share, feats), F32),
            dma,
            dma,
            dma,
            dma((3,)),
            dma((split - 1,)),
            dma((split - 1,)),
            dma,
            dma,
            dma,
            dma((heads,)),
            dma((3,)),
            dma((3,)),
            dma((REACH,)),
            dma((REACH,)),
            dma((REACH,)),
            dma((REACH,)),
        ]
        + [dma] * 8,
        compiler_params=pltpu.CompilerParams(
            collective_id=0, has_side_effects=True, vmem_limit_bytes=50 * 1024 * 1024
        ),
    )(stay(queries), stay(keys), stay(values), stay(seg), stay(feat_q), stay(key_map))

    errors, grad_keys, grad_q, grad_k = pl.pallas_call(
        functools.partial(store_kernel, 1.0 / math.sqrt(length * count)),
        name="store",
        out_shape=(
            shape((length, heads * width), BF16),
            shape((length, width), BF16),
            shape((count, per, feats), F32),
            shape((share, width // share, feats), F32),
        ),
        in_specs=[vmem] * 4,
        out_specs=[vmem] * 4,
        compiler_params=pltpu.CompilerParams(vmem_limit_bytes=8 * 1024 * 1024),
    )(*outs)
    return (
        errors,
        grad_keys,
        grad_q.reshape(heads, width, feats),
        grad_k.reshape(feat_k.shape),
    )


def solution(mesh):
    in_specs = (
        P(("dp", "context", "ulysses"), None),
        P(("dp", "context", "ulysses"), None),
        P(("dp", "context", "ulysses"), None),
        P(("dp", "context")),
        P("ulysses", None, None),
        P("ulysses", None, None),
    )
    out_specs = (
        P(("dp", "context"), "ulysses"),
        P(("dp", "context"), "ulysses"),
        P(("dp", "ulysses"), None, None),
        P(("dp", "ulysses"), None, None),
    )
    return jax.shard_map(
        on_device, mesh=mesh, in_specs=in_specs, out_specs=out_specs, check_vma=False
    )
```

time: 91.5 us -> 66.3 us (0.72)
  Pallas kernels: 86.5 us -> 65.5 us
  local copies, waits for them, and re-layouts: 4.1 us -> 0 us
    pallas_call x3 -> x2, Pallas kernels: 86.5 us -> 65.5 us  [the longest x1 64.2 us: on_device(): pl.pallas_call(step_kernel, name='step', out_shape=(shape((length, heads...]
    unnamed x5 -> x0, local copies, waits for them, and re-layouts: 4.1 us -> none
where the time goes in v2:
time: 66.3 us; the launch traced here: 66.1 us
  Pallas kernels  65.5 us (99%)
    pallas_call x1, Pallas kernels, on_device(): pl.pallas_call(step_kernel, name='step', out_shape=(shape((length, heads...  64.2 us

profile of v2, /device:TPU:2, one launch (start us, length us, event | category | flops | bytes accessed | tf_op | source)
XLA Modules:
  0.0 66.1 jit_solution(2409805606855929529)
XLA Ops:
  0.6 64.2 %step.1 = (bf16[512,1024]{1,0:T(8,128)(2,1)S(1)}, bf16[512,128]{1,0:T(8,128)(2,1)S(1)}, bf16[32,32,128]{2,1,0:T(8,128)(2,1)S(1)}, f32[16,8,128]{2,1,0:T(8,128)S(1)}) custom-call(bf16[128,4096]{1,0:T(8,128)(2,1)} %q_ref.1, bf16[128,512]{1,0:T(8,128)(2,1)} %k_ref.1, bf16[128,512]{1,0:T(8,128)(2,1)} %v_ref.1, s32[1,512]{1,0:T(1,128)} %bitcast.5, ...), custom_call_target="tpu_custom_call" | custom-call | tf_op jit(solution)/shard_map/step/pallas_call | solution.py:393
  64.8 1.3 %store.1 = (bf16[512,1024]{1,0:T(8,128)(2,1)}, bf16[512,128]{1,0:T(8,128)(2,1)}, f32[32,32,128]{2,1,0:T(8,128)}, f32[16,8,128]{2,1,0:T(8,128)}) custom-call(bf16[512,1024]{1,0:T(8,128)(2,1)S(1)} %get-tuple-element.12.err_in, bf16[512,128]{1,0:T(8,128)(2,1)S(1)} %get-tuple-element.13.keys_in, bf16[32,32,128]{2,1,0:T(8,128)(2,1)S(1)} %get-tuple-element.14.gq_in, ...), custom_call_target="tpu_custom_call" | custom-call | tf_op jit(solution)/shard_map/store/pallas_call | solution.py:462

commit v3 on v2

--- a/solution.py
+++ b/solution.py
@@ -71,9 +71,9 @@
     err_ref, keys_out, spread, kspread,
     seg_ref, qv, qb, kx, vx, fq, fk, rim_in, sbuf, rbuf, cbuf, dbuf,
     mask, bias, take, lead_s, phi_s, slope_s, num_s, den_s, tea_s, dn_s, dd_s, phik, slopek, dphik, cot, acc,
-    gq, part, red, kpart, kparts, kred,
+    gq, xin, zsend, zin, red, kpart, kxin, kmid, kzin, kred,
     ql, kl, vl, fl, ks, vs, qs, kr, vr, qr, rs, rr, xs, xr, cs, cr,
-    s1, r1, s2, r2, s3, r3, s4, r4,
+    s1, r1, s2, r2, s3, r3, s4, r4, s5, r5, s6, r6, s7, r7, ra,
 ):
     here, mine = lax.axis_index("context"), lax.axis_index("ulysses")
     count, split = lax.axis_size("context"), lax.axis_size("ulysses")
@@ -84,19 +84,24 @@
     step = 256
     inv_scale = 1.0 / math.sqrt(width)
 
+    share = count // heads
+    row, col_x = here // share, lax.rem(here, share)
+    planes = count // share
+
+    def beside(j):
+        return {"context": row * share + lax.rem(col_x + j, share)}
+
+    def along(j):
+        return {"context": lax.rem(row + j, planes) * share + col_x}
+
     barrier = pltpu.get_barrier_semaphore()
-    for j in range(1, split):
-        pl.semaphore_signal(
-            barrier, inc=1, device_id={"ulysses": lax.rem(mine + j, split)}, device_id_type=MESH
-        )
-
-    def greet(k, _):
-        pl.semaphore_signal(
-            barrier, inc=1, device_id={"context": lax.rem(here + k, count)}, device_id_type=MESH
-        )
-        return 0
-
-    lax.fori_loop(1, count, greet, 0)
+    near = [{"ulysses": lax.rem(mine + j, split)} for j in range(1, split)]
+    near += [beside(j) for j in range(1, share)]
+    near += [along(j) for j in range(1, planes)]
+    offsets = [k for k in range(-REACH, REACH + 1) if k]
+    near += [{"context": lax.rem(here + k + count, count)} for k in offsets]
+    for peer in near:
+        pl.semaphore_signal(barrier, inc=1, device_id=peer, device_id_type=MESH)
 
     def place(start):
         return pl.ds(pl.multiple_of(start + mine * rows, 128), rows)
@@ -114,6 +119,35 @@
     loads = [pltpu.make_async_copy(fq_ref, fq, fl.at[0]), pltpu.make_async_copy(fk_ref, fk, fl.at[1])]
     for copy in loads:
         copy.start()
+
+    pl.semaphore_wait(barrier, len(near))
+
+    sends = []
+    for src, dst, _, send, recv in small:
+        for j in range(1, split):
+            peer = lax.rem(mine + j, split)
+            copy = remote(
+                src.at[:, lanes(peer, width)], dst.at[place(WIN), :], send.at[j - 1], recv, ulysses=peer
+            )
+            copy.start()
+            sends.append(copy)
+
+    load_q.wait()
+    for h in range(heads):
+        pltpu.make_async_copy(
+            qv.at[:, lanes(mine * heads + h, width)], qb.at[h, place(0), :], qr.at[h]
+        ).start()
+
+    def send_q(h, _):
+        for j in range(1, split):
+            peer = lax.rem(mine + j, split)
+            remote(
+                qv.at[:, lanes(peer * heads + h, width)], qb.at[h, place(0), :], qs, qr.at[h],
+                ulysses=peer,
+            ).start()
+        return 0
+
+    lax.fori_loop(0, heads, send_q, 0)
 
     load_seg.wait()
     seg_row = seg_ref[...]
@@ -144,35 +178,6 @@
     cot[...] = jnp.zeros_like(cot)
     acc[...] = jnp.zeros_like(acc)
     dphik[...] = jnp.zeros_like(dphik)
-    load_q.wait()
-    for h in range(heads):
-        pltpu.make_async_copy(
-            qv.at[:, lanes(mine * heads + h, width)], qb.at[h, place(0), :], qr.at[h]
-        ).start()
-
-    pl.semaphore_wait(barrier, split - 1 + count - 1)
-
-    sends = []
-    for src, dst, _, send, recv in small:
-        for j in range(1, split):
-            peer = lax.rem(mine + j, split)
-            copy = remote(
-                src.at[:, lanes(peer, width)], dst.at[place(WIN), :], send.at[j - 1], recv, ulysses=peer
-            )
-            copy.start()
-            sends.append(copy)
-
-    def send_q(h, _):
-        for j in range(1, split):
-            peer = lax.rem(mine + j, split)
-            remote(
-                qv.at[:, lanes(peer * heads + h, width)], qb.at[h, place(0), :], qs, qr.at[h],
-                ulysses=peer,
-            ).start()
-        return 0
-
-    lax.fori_loop(0, heads, send_q, 0)
-
     for copy in loads:
         copy.wait()
     whole(kx.at[pl.ds(WIN, length), :], kr).wait()
@@ -269,29 +274,21 @@
         sends.append(copy)
 
     per = gq.shape[1]
-    share = width // per
-
-    def head_of(s):
-        return lax.rem(s + here // share, heads)
-
-    def scatter(s):
-        for j in range(share):
-            owner = head_of(s) * share + j
-
-            @pl.when(owner != here)
-            def _():
-                remote(gq.at[owner], part.at[here], s1, r1, context=owner).start()
-
-            @pl.when(owner == here)
-            def _():
-                pltpu.make_async_copy(gq.at[owner], part.at[here], r1).start()
-
-    def backward(s, _):
-        h = head_of(s)
-
-        @pl.when(s > 0)
+
+    def scatter(h):
+        pltpu.make_async_copy(gq.at[h * share + col_x], xin.at[col_x, h], r1).start()
+        for j in range(1, share):
+            to = h * share + lax.rem(col_x + j, share)
+            peer = beside(j)
+            pltpu.make_async_remote_copy(
+                src_ref=gq.at[to], dst_ref=xin.at[col_x, h], send_sem=s1, recv_sem=r1,
+                device_id=peer, device_id_type=MESH,
+            ).start()
+
+    def backward(h, _):
+        @pl.when(h > 0)
         def _():
-            scatter(s - 1)
+            scatter(h - 1)
 
         outs = []
         for i in range(0, length, step):
@@ -319,57 +316,81 @@
     d_phi = dphik[...] + own * (dot_nt(vx[WIN : WIN + length, :], back.astype(BF16)) + back_norm)
     d_pre = (d_phi * slopek[...]).astype(BF16)
     grad = dot_tn(kx[WIN : WIN + length, :], d_pre)
-    kpart[...] = grad.reshape(kpart.shape)
-
-    pltpu.make_async_copy(kpart.at[here // 2], kparts.at[here], r3).start()
-
-    def scatter_k(k, _):
-        peer = lax.rem(here + k, count)
-        remote(kpart.at[peer // 2], kparts.at[here], s3, r3, context=peer).start()
-        return 0
-
-    lax.fori_loop(1, count, scatter_k, 0)
+    kpart[...] = grad.reshape(kpart.shape).astype(BF16)
+
+    def send(src, dst, send_sem, recv_sem, peer):
+        pltpu.make_async_remote_copy(
+            src_ref=src, dst_ref=dst, send_sem=send_sem, recv_sem=recv_sem,
+            device_id=peer, device_id_type=MESH,
+        ).start()
+
+    def piece(ref, peer):
+        return ref.at[lax.rem(peer["context"], share)]
+
+    pltpu.make_async_copy(kpart.at[col_x], kxin.at[col_x], r4).start()
+    for j in range(1, share):
+        send(piece(kpart, beside(j)), kxin.at[col_x], s4, r4, beside(j))
     keys_out[...] = dot_nt(d_pre, fk[...]).astype(BF16)
 
-    whole(part, r1).wait()
-    red[...] = jnp.sum(part[...].astype(F32), axis=0).astype(BF16)
-    pltpu.make_async_copy(red, spread.at[here], r2).start()
-
-    def spread_q(k, _):
-        peer = lax.rem(here + k, count)
-        remote(red, spread.at[here], s2, r2, context=peer).start()
-        return 0
-
-    lax.fori_loop(1, count, spread_q, 0)
-
-    whole(kparts, r3).wait()
-    kred[...] = jnp.sum(kparts[...], axis=0)
-    pltpu.make_async_copy(kred, kspread.at[here // 2], r4).start()
-
-    def spread_k(k, _):
-        peer = lax.rem(here + 2 * k, count)
-        remote(kred, kspread.at[here // 2], s4, r4, context=peer).start()
-        return 0
-
-    lax.fori_loop(1, count // 2, spread_k, 0)
+    whole(xin, r1).wait()
+    zsend[...] = jnp.sum(xin[...].astype(F32), axis=0).astype(BF16)
+    pltpu.make_async_copy(zsend.at[row], zin.at[row], r2).start()
+    for j in range(1, planes):
+        send(zsend.at[lax.rem(row + j, planes)], zin.at[row], s2, r2, along(j))
+
+    whole(kxin, r4).wait()
+    kmid[...] = jnp.sum(kxin[...].astype(F32), axis=0).astype(BF16)
+    pltpu.make_async_copy(kmid, kzin.at[row], r5).start()
+    for j in range(1, planes):
+        send(kmid, kzin.at[row], s5, r5, along(j))
+
+    whole(zin, r2).wait()
+    red[...] = jnp.sum(zin[...].astype(F32), axis=0).astype(BF16)
+    pltpu.make_async_copy(red, spread.at[here], r3).start()
+    for j in range(1, planes):
+        send(red, spread.at[here], s3, ra.at[row], along(j))
+    for j in range(1, share):
+        send(red, spread.at[here], s7, r7, beside(j))
+
+    def pass_on(off):
+        source = lax.rem(row + off, planes)
+        chunk = spread.at[source * share + col_x]
+        whole(chunk, ra.at[source]).wait()
+        for j in range(1, share):
+            send(chunk, chunk, s7, r7, beside(j))
+
+    order = sorted(range(1, planes), key=lambda o: min(o, planes - o))
+    for off in order[:-3]:
+        pass_on(off)
+    whole(kzin, r5).wait()
+    kred[...] = jnp.sum(kzin[...].astype(F32), axis=0).astype(BF16)
+    pltpu.make_async_copy(kred, kspread.at[col_x], r6).start()
+    for j in range(1, share):
+        send(kred, kspread.at[col_x], s6, r6, beside(j))
+    for off in order[-3:]:
+        pass_on(off)
 
     for copy in sends:
         copy.wait_send()
     whole(qb.at[:, pl.ds(0, length - rows), :], qs).wait()
-    rest = pl.ds(0, count - 1)
-    whole(part.at[rest], s1).wait()
-    whole(kparts.at[rest], s3).wait()
-    whole(spread.at[rest], s2).wait()
-    whole(kspread.at[pl.ds(0, count // 2 - 1)], s4).wait()
-    whole(spread, r2).wait()
-    whole(kspread, r4).wait()
+    whole(xin.at[pl.ds(0, share - 1)], s1).wait()
+    whole(zin.at[pl.ds(0, planes - 1)], s2).wait()
+    whole(spread.at[pl.ds(0, planes - 1)], s3).wait()
+    whole(kxin.at[pl.ds(0, share - 1)], s4).wait()
+    whole(kzin.at[pl.ds(0, planes - 1)], s5).wait()
+    whole(kspread.at[pl.ds(0, share - 1)], s6).wait()
+    beyond = spread.at[pl.ds(0, (share - 1) * planes)]
+    whole(beyond, s7).wait()
+    whole(spread.at[here], r3).wait()
+    whole(kspread, r6).wait()
+    whole(beyond, r7).wait()
 
 
 def store_kernel(scale, err_in, keys_in, gq_in, gk_in, err_out, keys_out, gq_out, gk_out):
     err_out[...] = err_in[...]
     keys_out[...] = keys_in[...]
     gq_out[...] = gq_in[...].astype(F32) * scale
-    gk_out[...] = gk_in[...] * scale
+    gk_out[...] = gk_in[...].astype(F32) * scale
 
 
 def on_device(queries, keys, values, segments, feat_q, feat_k):
@@ -381,7 +402,8 @@
     seg = segments.reshape(1, length)
     key_map = feat_k.reshape(width, feats)
     per = heads * width // count
-    share = count // 2
+    share = count // heads
+    planes = count // share
     shape = jax.ShapeDtypeStruct
     hbm = pl.BlockSpec(memory_space=pltpu.HBM)
     vmem = pl.BlockSpec(memory_space=pltpu.VMEM)
@@ -397,7 +419,7 @@
             shape((length, heads * width), BF16),
             shape((length, width), BF16),
             shape((count, per, feats), BF16),
-            shape((share, width // share, feats), F32),
+            shape((share, width // share, feats), BF16),
         ),
         in_specs=[hbm] * 6,
         out_specs=[vmem] * 4,
@@ -431,11 +453,15 @@
             pltpu.VMEM((feats, width), F32),
             pltpu.VMEM((8, feats), F32),
             pltpu.VMEM((count, per, feats), BF16),
-            pltpu.VMEM((count, per, feats), BF16),
+            pltpu.VMEM((share, planes, per, feats), BF16),
+            pltpu.VMEM((planes, per, feats), BF16),
+            pltpu.VMEM((planes, per, feats), BF16),
             pltpu.VMEM((per, feats), BF16),
-            pltpu.VMEM((share, width // share, feats), F32),
-            pltpu.VMEM((count, width // share, feats), F32),
-            pltpu.VMEM((width // share, feats), F32),
+            pltpu.VMEM((share, per, feats), BF16),
+            pltpu.VMEM((share, per, feats), BF16),
+            pltpu.VMEM((per, feats), BF16),
+            pltpu.VMEM((planes, per, feats), BF16),
+            pltpu.VMEM((per, feats), BF16),
             dma,
             dma,
             dma,
@@ -453,7 +479,8 @@
             dma((REACH,)),
             dma((REACH,)),
         ]
-        + [dma] * 8,
+        + [dma] * 14
+        + [dma((planes,))],
         compiler_params=pltpu.CompilerParams(
             collective_id=0, has_side_effects=True, vmem_limit_bytes=50 * 1024 * 1024
         ),

time: 66.3 us -> 59.4 us (0.90)
  Pallas kernels: 65.5 us -> 58.3 us
    pallas_call x1, Pallas kernels: 64.2 us -> 57 us  [on_device(): pl.pallas_call(step_kernel, name='step', out_shape=(shape((length, heads...]
where the time goes in v3:
time: 59.4 us; the launch traced here: 59 us
  Pallas kernels  58.3 us (98%)
  between operations  0.64 us (1%)
    pallas_call x1, Pallas kernels, on_device(): pl.pallas_call(step_kernel, name='step', out_shape=(shape((length, heads...  57 us
    pallas_call x1, Pallas kernels, on_device(): pl.pallas_call(functools.partial(store_kernel, 1.0 / math.sqrt(length * c...  1.28 us

profile of v3, /device:TPU:2, one launch (start us, length us, event | category | flops | bytes accessed | tf_op | source)
XLA Modules:
  0.0 59.0 jit_solution(15241665853438196630)
XLA Ops:
  0.6 57.0 %step.1 = (bf16[512,1024]{1,0:T(8,128)(2,1)S(1)}, bf16[512,128]{1,0:T(8,128)(2,1)S(1)}, bf16[32,32,128]{2,1,0:T(8,128)(2,1)S(1)}, bf16[4,32,128]{2,1,0:T(8,128)(2,1)S(1)}) custom-call(bf16[128,4096]{1,0:T(8,128)(2,1)} %q_ref.1, bf16[128,512]{1,0:T(8,128)(2,1)} %k_ref.1, bf16[128,512]{1,0:T(8,128)(2,1)} %v_ref.1, s32[1,512]{1,0:T(1,128)} %bitcast.5, ...), custom_call_target="tpu_custom_call" | custom-call | tf_op jit(solution)/shard_map/step/pallas_call | solution.py:415
  57.7 1.3 %store.1 = (bf16[512,1024]{1,0:T(8,128)(2,1)}, bf16[512,128]{1,0:T(8,128)(2,1)}, f32[32,32,128]{2,1,0:T(8,128)}, f32[4,32,128]{2,1,0:T(8,128)}) custom-call(bf16[512,1024]{1,0:T(8,128)(2,1)S(1)} %get-tuple-element.12.err_in, bf16[512,128]{1,0:T(8,128)(2,1)S(1)} %get-tuple-element.13.keys_in, bf16[32,32,128]{2,1,0:T(8,128)(2,1)S(1)} %get-tuple-element.14.gq_in, ...), custom_call_target="tpu_custom_call" | custom-call | tf_op jit(solution)/shard_map/store/pallas_call | solution.py:489

commit v4 on v3

--- a/solution.py
+++ b/solution.py
@@ -10,6 +10,7 @@
 
 WIN = 128
 REACH = 8
+SPLIT = 4
 TAIL = 16
 MESH = pl.DeviceIdType.MESH
 F32 = jnp.float32
@@ -69,10 +70,10 @@
 def step_kernel(
     q_ref, k_ref, v_ref, seg_in, fq_ref, fk_ref,
     err_ref, keys_out, spread, kspread,
-    seg_ref, qv, qb, kx, vx, fq, fk, rim_in, sbuf, rbuf, cbuf, dbuf,
-    mask, bias, take, lead_s, phi_s, slope_s, num_s, den_s, tea_s, dn_s, dd_s, phik, slopek, dphik, cot, acc,
+    seg_ref, qv, qb, kx, vx, fq, fk, rim_in, sbuf, rbuf, cbuf, dbuf, tbuf, ebuf, back_s, backn_s,
+    mask, bias, take, takeb, lead_s, phi_s, slope_s, num_s, den_s, tea_s, dn_s, dd_s, phik, slopek, dphik, cot, acc,
     gq, xin, zsend, zin, red, kpart, kxin, kmid, kzin, kred,
-    ql, kl, vl, fl, ks, vs, qs, kr, vr, qr, rs, rr, xs, xr, cs, cr,
+    ql, fl, ks, vs, qs, kr, vr, qr, rs, rr, xs, xr, cs, cr, es, er,
     s1, r1, s2, r2, s3, r3, s4, r4, s5, r5, s6, r6, s7, r7, ra,
 ):
     here, mine = lax.axis_index("context"), lax.axis_index("ulysses")
@@ -111,9 +112,12 @@
 
     load_seg = pltpu.make_async_copy(seg_in, seg_ref, fl.at[2])
     load_seg.start()
-    small = ((k_ref, kx, kl, ks, kr), (v_ref, vx, vl, vs, vr))
-    for src, dst, _, _, recv in small:
-        pltpu.make_async_copy(src.at[:, lanes(mine, width)], dst.at[place(WIN), :], recv).start()
+    front = pl.ds(0, width)
+    small = ((k_ref, kx, ks, kr), (v_ref, vx, vs, vr))
+    for src, dst, _, recv in small:
+        pltpu.make_async_copy(
+            src.at[:, lanes(mine, width)], dst.at[place(WIN), front], recv.at[mine]
+        ).start()
     load_q = pltpu.make_async_copy(q_ref, qv, ql)
     load_q.start()
     loads = [pltpu.make_async_copy(fq_ref, fq, fl.at[0]), pltpu.make_async_copy(fk_ref, fk, fl.at[1])]
@@ -123,11 +127,12 @@
     pl.semaphore_wait(barrier, len(near))
 
     sends = []
-    for src, dst, _, send, recv in small:
+    for src, dst, send, recv in small:
         for j in range(1, split):
             peer = lax.rem(mine + j, split)
             copy = remote(
-                src.at[:, lanes(peer, width)], dst.at[place(WIN), :], send.at[j - 1], recv, ulysses=peer
+                src.at[:, lanes(peer, width)], dst.at[place(WIN), front], send.at[j - 1],
+                recv.at[mine], ulysses=peer,
             )
             copy.start()
             sends.append(copy)
@@ -156,6 +161,7 @@
     last_id = jnp.max(seg_row, axis=1, keepdims=True).astype(F32)
     seg_col = columns_of(seg_row)
     take[...] = jnp.where(seg_col == first_id, 1.0, 0.0)
+    takeb[...] = jnp.where(seg_col == first_id, 1.0, 0.0).astype(BF16)
     r = lax.broadcasted_iota(jnp.int32, (128, 128), 0)
     c = lax.broadcasted_iota(jnp.int32, (128, 128), 1)
     for i in range(0, length, 128):
@@ -180,17 +186,26 @@
     dphik[...] = jnp.zeros_like(dphik)
     for copy in loads:
         copy.wait()
-    whole(kx.at[pl.ds(WIN, length), :], kr).wait()
-    whole(vx.at[pl.ds(WIN, length), :], vr).wait()
     after = lax.rem(here + 1, count)
     edge, rim = pl.ds(length, WIN), pl.ds(0, WIN)
     rims = [
-        remote(kx.at[edge, :], kx.at[rim, :], rs.at[0], rr.at[0], context=after),
-        remote(vx.at[edge, :], vx.at[rim, :], rs.at[1], rr.at[1], context=after),
         remote(seg_ref.at[:, pl.ds(length - WIN, WIN)], rim_in, rs.at[2], rr.at[2], context=after),
+        remote(kx.at[edge, front], kx.at[rim, front], rs.at[0], rr.at[0], context=after),
+        remote(vx.at[edge, front], vx.at[rim, front], rs.at[1], rr.at[1], context=after),
     ]
-    for copy in rims:
-        copy.start()
+    rims[0].start()
+
+    def arrived(ref, sems, who):
+        whole(ref.at[pl.ds(WIN + who * rows, rows), front], sems.at[who]).wait()
+
+    arrived(kx, kr, split - 1)
+    rims[1].start()
+    arrived(vx, vr, split - 1)
+    rims[2].start()
+    for who in range(split - 1):
+        arrived(kx, kr, who)
+    for who in range(split - 1):
+        arrived(vx, vr, who)
 
     pre = dot_nn(kx[WIN : WIN + length, :], fk[...])
     low = jnp.exp(jnp.minimum(pre, 0.0))
@@ -199,7 +214,7 @@
     slopek[...] = jnp.where(pre > 0, 1.0, low)
     tail = jnp.where(seg_col == last_id, phi.astype(F32), 0.0)
     state, end = payload(
-        dot_tn(tail.astype(BF16), vx[WIN : WIN + length, :]),
+        dot_tn(tail.astype(BF16), vx[WIN : WIN + length, 0:width]),
         jnp.sum(tail, axis=0, keepdims=True),
         last_id,
     )
@@ -223,7 +238,7 @@
         phi = jnp.where(pre > 0, pre + 1.0, low).astype(BF16)
         slope_s[h] = jnp.where(pre > 0, 1.0, low)
         phi_s[h] = phi
-        lead_s[h] = (phi.astype(F32) * take[...]).astype(BF16)
+        lead_s[h] = phi * takeb[...]
         for i in range(0, length, step):
             end = i + step
             score = dot_nt(phi[i:end], phik[0:end, :]) * mask[i:end, 0:end]
@@ -234,7 +249,9 @@
                 logits += bias[j : j + 128, :]
                 probs = jnp.exp(logits - jnp.max(logits, axis=1, keepdims=True))
                 total = jnp.sum(probs, axis=1, keepdims=True)
-                tea_s[h, j : j + 128, :] = dot_nn(probs.astype(BF16), vx[j : j + 256, :]) / total
+                tea_s[h, j : j + 128, :] = dot_nn(probs.astype(BF16), vx[j : j + 256, :]) * (
+                    1.0 / total
+                )
         return 0
 
     lax.fori_loop(0, heads, forward, 0)
@@ -247,10 +264,8 @@
     def meet(h, _):
         lead = lead_s[h]
         lead_f = lead.astype(F32)
-        numer = num_s[h] + dot_nn(lead, state)
-        denom = den_s[h] + jnp.sum(lead_f * norm, axis=1, keepdims=True)
-        inv = 1.0 / denom
-        student = numer * inv
+        inv = 1.0 / (den_s[h] + jnp.sum(lead_f * norm, axis=1, keepdims=True))
+        student = (num_s[h] + dot_nn(lead, state)) * inv
         gap = student - tea_s[h]
         err_ref[:, lanes(h, width)] = gap.astype(BF16)
         up = 32.0 * gap
@@ -262,33 +277,78 @@
         cot[...] += dot_tn(lead, dn)
         return 0
 
-    lax.fori_loop(0, heads, meet, 0)
+    def meet_two(t, _):
+        meet(2 * t, 0)
+        return meet(2 * t + 1, 0)
+
+    lax.fori_loop(0, heads // 2, meet_two, 0)
     total, end = payload(cot[...], jnp.sum(acc[...], axis=0, keepdims=True), first_id)
     cbuf[0:feats, :] = total
     cbuf[feats : feats + TAIL, :] = end
-    for k in range(REACH):
-        copy = remote(
-            cbuf, dbuf.at[k], cs.at[k], cr.at[k], context=lax.rem(here + count - k - 1, count)
-        )
-        copy.start()
-        sends.append(copy)
+
+    def send(src, dst, send_sem, recv_sem, peer):
+        pltpu.make_async_remote_copy(
+            src_ref=src, dst_ref=dst, send_sem=send_sem, recv_sem=recv_sem,
+            device_id=peer, device_id_type=MESH,
+        ).start()
+
+    for j in range(1, share):
+        send(cbuf, dbuf.at[j - 1], cs, cr.at[j - 1], beside(j))
+
+    def opened(buf, slot):
+        tail = buf[slot, feats : feats + TAIL, :].astype(F32)
+        return buf[slot, 0:feats, :].astype(F32), tail[0:1, :], tail[1:2, :]
+
+    def join_row():
+        for j in range(share - 1):
+            whole(dbuf.at[j], cr.at[j]).wait()
+        parts = [opened(dbuf, j) for j in range(share - 1)]
+        mine_norm = cbuf[feats : feats + TAIL, :].astype(F32)
+        parts.append((cbuf[0:feats, :].astype(F32), mine_norm[0:1, :], mine_norm[1:2, :]))
+        lead_id = parts[0][2]
+        for part in parts[1:]:
+            lead_id = jnp.minimum(lead_id, part[2])
+        sums = [jnp.where(p[2] == lead_id, p[0], 0.0) for p in parts]
+        norms = [jnp.where(p[2] == lead_id, p[1], 0.0) for p in parts]
+        total, end = payload(sum(sums), sum(norms), lead_id)
+        tbuf[0:feats, :] = total
+        tbuf[feats : feats + TAIL, :] = end
+        for k in range(2):
+            send(tbuf, ebuf.at[k], es, er.at[k], along(planes - 1 - k))
+        back, back_norm = jnp.zeros((feats, width), F32), jnp.zeros((1, feats), F32)
+        for j in range(share - 1):
+            source = lax.rem(col_x + share - 1 - j, share)
+            keep = (parts[j][2] == last_id) & (source > col_x)
+            back += jnp.where(keep, parts[j][0], 0.0)
+            back_norm += jnp.where(keep, parts[j][1], 0.0)
+        back_s[...] = back
+        backn_s[...] = jnp.broadcast_to(back_norm, backn_s.shape)
 
     per = gq.shape[1]
 
-    def scatter(h):
-        pltpu.make_async_copy(gq.at[h * share + col_x], xin.at[col_x, h], r1).start()
+    def head_of(turn):
+        off = ((planes - turn) // 2) * (2 * (turn % 2) - 1)
+        return lax.rem(row + off + planes, planes)
+
+    def scatter(turn):
+        h = head_of(turn)
+        pltpu.make_async_copy(gq.at[h * share + col_x], xin.at[h, col_x], r1.at[h]).start()
         for j in range(1, share):
             to = h * share + lax.rem(col_x + j, share)
-            peer = beside(j)
-            pltpu.make_async_remote_copy(
-                src_ref=gq.at[to], dst_ref=xin.at[col_x, h], send_sem=s1, recv_sem=r1,
-                device_id=peer, device_id_type=MESH,
-            ).start()
-
-    def backward(h, _):
-        @pl.when(h > 0)
-        def _():
-            scatter(h - 1)
+            send(gq.at[to], xin.at[h, col_x], s1, r1.at[h], beside(j))
+
+    def row_sum(turn):
+        h = head_of(turn)
+        whole(xin.at[h], r1.at[h]).wait()
+        return h, jnp.sum(xin[h].astype(F32), axis=0).astype(BF16)
+
+    def climb(turn):
+        h, part = row_sum(turn)
+        zsend[h] = part
+        send(zsend.at[h], zin.at[row], s2, r2, {"context": h * share + col_x})
+
+    def backward(turn, _):
+        h = head_of(turn)
 
         outs = []
         for i in range(0, length, step):
@@ -306,23 +366,35 @@
             gq[h * share + j] = grad[j * per : (j + 1) * per, :]
         return 0
 
-    lax.fori_loop(0, heads, backward, 0)
-    scatter(heads - 1)
-
-    for k in range(REACH):
-        whole(dbuf.at[k], cr.at[k]).wait()
-    back, back_norm = gathered(dbuf, last_id, here, count, False)
+    def backward_two(t, _):
+        backward(2 * t, 0)
+        return backward(2 * t + 1, 0)
+
+    lax.fori_loop(0, SPLIT // 2, backward_two, 0)
+    join_row()
+    for turn in range(SPLIT):
+        scatter(turn)
+    backward_two(SPLIT // 2, 0)
+    scatter(SPLIT)
+    scatter(SPLIT + 1)
+    backward_two(SPLIT // 2 + 1, 0)
+    scatter(SPLIT + 2)
+    scatter(SPLIT + 3)
+    for turn in range(SPLIT - 1):
+        climb(turn)
+
+    back, back_norm = back_s[...], backn_s[0:1, :]
+    for k in range(2):
+        whole(ebuf.at[k], er.at[k]).wait()
+        part = opened(ebuf, k)
+        keep = (part[2] == last_id) & (row + k + 1 < planes)
+        back += jnp.where(keep, part[0], 0.0)
+        back_norm += jnp.where(keep, part[1], 0.0)
     own = jnp.where(columns_of(seg_ref[...]) == last_id, 1.0, 0.0)
-    d_phi = dphik[...] + own * (dot_nt(vx[WIN : WIN + length, :], back.astype(BF16)) + back_norm)
+    d_phi = dphik[...] + own * (dot_nt(vx[WIN : WIN + length, 0:width], back.astype(BF16)) + back_norm)
     d_pre = (d_phi * slopek[...]).astype(BF16)
     grad = dot_tn(kx[WIN : WIN + length, :], d_pre)
     kpart[...] = grad.reshape(kpart.shape).astype(BF16)
-
-    def send(src, dst, send_sem, recv_sem, peer):
-        pltpu.make_async_remote_copy(
-            src_ref=src, dst_ref=dst, send_sem=send_sem, recv_sem=recv_sem,
-            device_id=peer, device_id_type=MESH,
-        ).start()
 
     def piece(ref, peer):
         return ref.at[lax.rem(peer["context"], share)]
@@ -332,19 +404,15 @@
         send(piece(kpart, beside(j)), kxin.at[col_x], s4, r4, beside(j))
     keys_out[...] = dot_nt(d_pre, fk[...]).astype(BF16)
 
-    whole(xin, r1).wait()
-    zsend[...] = jnp.sum(xin[...].astype(F32), axis=0).astype(BF16)
-    pltpu.make_async_copy(zsend.at[row], zin.at[row], r2).start()
-    for j in range(1, planes):
-        send(zsend.at[lax.rem(row + j, planes)], zin.at[row], s2, r2, along(j))
-
+    for turn in range(SPLIT - 1, heads - 1):
+        climb(turn)
+    zin[row] = row_sum(heads - 1)[1]
     whole(kxin, r4).wait()
     kmid[...] = jnp.sum(kxin[...].astype(F32), axis=0).astype(BF16)
     pltpu.make_async_copy(kmid, kzin.at[row], r5).start()
     for j in range(1, planes):
         send(kmid, kzin.at[row], s5, r5, along(j))
-
-    whole(zin, r2).wait()
+    whole(zin.at[pl.ds(0, planes - 1)], r2).wait()
     red[...] = jnp.sum(zin[...].astype(F32), axis=0).astype(BF16)
     pltpu.make_async_copy(red, spread.at[here], r3).start()
     for j in range(1, planes):
@@ -373,7 +441,9 @@
     for copy in sends:
         copy.wait_send()
     whole(qb.at[:, pl.ds(0, length - rows), :], qs).wait()
-    whole(xin.at[pl.ds(0, share - 1)], s1).wait()
+    whole(dbuf, cs).wait()
+    whole(ebuf, es).wait()
+    whole(xin.at[:, pl.ds(0, share - 1)], s1).wait()
     whole(zin.at[pl.ds(0, planes - 1)], s2).wait()
     whole(spread.at[pl.ds(0, planes - 1)], s3).wait()
     whole(kxin.at[pl.ds(0, share - 1)], s4).wait()
@@ -435,10 +505,15 @@
             pltpu.VMEM((packed, width), BF16),
             pltpu.VMEM((REACH, packed, width), BF16),
             pltpu.VMEM((packed, width), BF16),
-            pltpu.VMEM((REACH, packed, width), BF16),
+            pltpu.VMEM((share - 1, packed, width), BF16),
+            pltpu.VMEM((packed, width), BF16),
+            pltpu.VMEM((2, packed, width), BF16),
+            pltpu.VMEM((feats, width), F32),
+            pltpu.VMEM((8, feats), F32),
             pltpu.VMEM((length, length), F32),
             pltpu.VMEM((length, 2 * WIN), F32),
             pltpu.VMEM((length, feats), F32),
+            pltpu.VMEM((length, feats), BF16),
             pltpu.VMEM((heads, length, feats), BF16),
             pltpu.VMEM((heads, length, feats), BF16),
             pltpu.VMEM((heads, length, feats), F32),
@@ -453,7 +528,7 @@
             pltpu.VMEM((feats, width), F32),
             pltpu.VMEM((8, feats), F32),
             pltpu.VMEM((count, per, feats), BF16),
-            pltpu.VMEM((share, planes, per, feats), BF16),
+            pltpu.VMEM((planes, share, per, feats), BF16),
             pltpu.VMEM((planes, per, feats), BF16),
             pltpu.VMEM((planes, per, feats), BF16),
             pltpu.VMEM((per, feats), BF16),
@@ -463,23 +538,24 @@
             pltpu.VMEM((planes, per, feats), BF16),
             pltpu.VMEM((per, feats), BF16),
             dma,
-            dma,
-            dma,
             dma((3,)),
             dma((split - 1,)),
             dma((split - 1,)),
             dma,
-            dma,
-            dma,
+            dma((split,)),
+            dma((split,)),
             dma((heads,)),
             dma((3,)),
             dma((3,)),
             dma((REACH,)),
             dma((REACH,)),
-            dma((REACH,)),
-            dma((REACH,)),
+            dma,
+            dma((share - 1,)),
+            dma,
+            dma((2,)),
         ]
-        + [dma] * 14
+        + [dma, dma((heads,))]
+        + [dma] * 12
         + [dma((planes,))],
         compiler_params=pltpu.CompilerParams(
             collective_id=0, has_side_effects=True, vmem_limit_bytes=50 * 1024 * 1024

time: 59.4 us -> 56.5 us (0.951)
  Pallas kernels: 58.3 us -> 55.3 us
    pallas_call x1, Pallas kernels: 57 us -> 54.1 us  [on_device(): pl.pallas_call(step_kernel, name='step', out_shape=(shape((length, heads...]
where the time goes in v4:
time: 56.5 us; the launch traced here: 56 us
  Pallas kernels  55.3 us (98%)
  between operations  0.64 us (1%)
    pallas_call x1, Pallas kernels, on_device(): pl.pallas_call(step_kernel, name='step', out_shape=(shape((length, heads...  54.1 us
    pallas_call x1, Pallas kernels, on_device(): pl.pallas_call(functools.partial(store_kernel, 1.0 / math.sqrt(length * c...  1.28 us

profile of v4, /device:TPU:2, one launch (start us, length us, event | category | flops | bytes accessed | tf_op | source)
XLA Modules:
  0.0 56.0 jit_solution(9896305131839635525)
XLA Ops:
  0.6 54.1 %step.1 = (bf16[512,1024]{1,0:T(8,128)(2,1)S(1)}, bf16[512,128]{1,0:T(8,128)(2,1)S(1)}, bf16[32,32,128]{2,1,0:T(8,128)(2,1)S(1)}, bf16[4,32,128]{2,1,0:T(8,128)(2,1)S(1)}) custom-call(bf16[128,4096]{1,0:T(8,128)(2,1)} %q_ref.1, bf16[128,512]{1,0:T(8,128)(2,1)} %k_ref.1, bf16[128,512]{1,0:T(8,128)(2,1)} %v_ref.1, s32[1,512]{1,0:T(1,128)} %bitcast.5, ...), custom_call_target="tpu_custom_call" | custom-call | tf_op jit(solution)/shard_map/step/pallas_call | solution.py:485
  54.7 1.3 %store.1 = (bf16[512,1024]{1,0:T(8,128)(2,1)}, bf16[512,128]{1,0:T(8,128)(2,1)}, f32[32,32,128]{2,1,0:T(8,128)}, f32[4,32,128]{2,1,0:T(8,128)}) custom-call(bf16[512,1024]{1,0:T(8,128)(2,1)S(1)} %get-tuple-element.12.err_in, bf16[512,128]{1,0:T(8,128)(2,1)S(1)} %get-tuple-element.13.keys_in, bf16[32,32,128]{2,1,0:T(8,128)(2,1)S(1)} %get-tuple-element.14.gq_in, ...), custom_call_target="tpu_custom_call" | custom-call | tf_op jit(solution)/shard_map/store/pallas_call | solution.py:565

commit v5 on v4

--- a/solution.py
+++ b/solution.py
@@ -9,7 +9,7 @@
 from jax.sharding import PartitionSpec as P
 
 WIN = 128
-REACH = 8
+JOIN = 3
 SPLIT = 4
 TAIL = 16
 MESH = pl.DeviceIdType.MESH
@@ -54,26 +54,13 @@
     return state.astype(BF16), tail.astype(BF16)
 
 
-def gathered(buf, ident, here, count, forward):
-    feats = buf.shape[1] - TAIL
-    state = jnp.zeros((feats, buf.shape[2]), F32)
-    norm = jnp.zeros((1, buf.shape[2]), F32)
-    for k in range(REACH):
-        inside = here > k if forward else here + k + 1 < count
-        tail = buf[k, feats : feats + TAIL, :].astype(F32)
-        keep = (tail[1:2, :] == ident) & inside
-        state += jnp.where(keep, buf[k, 0:feats, :].astype(F32), 0.0)
-        norm += jnp.where(keep, tail[0:1, :], 0.0)
-    return state, norm
-
-
 def step_kernel(
     q_ref, k_ref, v_ref, seg_in, fq_ref, fk_ref,
     err_ref, keys_out, spread, kspread,
-    seg_ref, qv, qb, kx, vx, fq, fk, rim_in, sbuf, rbuf, cbuf, dbuf, tbuf, ebuf, back_s, backn_s,
+    seg_ref, qv, qb, kx, vx, fq, fk, rim_in, sbuf, rbuf, cbuf, dbuf, tbuf, ebuf, ubuf, wbuf, back_s, backn_s,
     mask, bias, take, takeb, lead_s, phi_s, slope_s, num_s, den_s, tea_s, dn_s, dd_s, phik, slopek, dphik, cot, acc,
     gq, xin, zsend, zin, red, kpart, kxin, kmid, kzin, kred,
-    ql, fl, ks, vs, qs, kr, vr, qr, rs, rr, xs, xr, cs, cr, es, er,
+    ql, fl, ks, vs, qs, kr, vr, qr, rs, rr, xs, xr, cs, cr, es, er, us, ur,
     s1, r1, s2, r2, s3, r3, s4, r4, s5, r5, s6, r6, s7, r7, ra,
 ):
     here, mine = lax.axis_index("context"), lax.axis_index("ulysses")
@@ -99,8 +86,7 @@
     near = [{"ulysses": lax.rem(mine + j, split)} for j in range(1, split)]
     near += [beside(j) for j in range(1, share)]
     near += [along(j) for j in range(1, planes)]
-    offsets = [k for k in range(-REACH, REACH + 1) if k]
-    near += [{"context": lax.rem(here + k + count, count)} for k in offsets]
+    near += [{"context": lax.rem(here + k, count)} for k in (1, count - 1)]
     for peer in near:
         pl.semaphore_signal(barrier, inc=1, device_id=peer, device_id_type=MESH)
 
@@ -220,18 +206,56 @@
     )
     sbuf[0:feats, :] = state
     sbuf[feats : feats + TAIL, :] = end
-    for k in range(REACH):
-        copy = remote(sbuf, rbuf.at[k], xs.at[k], xr.at[k], context=lax.rem(here + k + 1, count))
-        copy.start()
-        sends.append(copy)
-
-    for copy in rims:
-        copy.wait()
-    rim_f = jnp.where(here > 0, rim_in[...], -1).astype(F32)
-    bias[0:128, 0:128] = jnp.where((seg_col[0:128, :] == rim_f) & (c > r), 0.0, -1e30)
-
-    def forward(h, _):
-        whole(qb.at[h], qr.at[h]).wait()
+    def send(src, dst, send_sem, recv_sem, peer):
+        pltpu.make_async_remote_copy(
+            src_ref=src, dst_ref=dst, send_sem=send_sem, recv_sem=recv_sem,
+            device_id=peer, device_id_type=MESH,
+        ).start()
+
+    def opened(ref):
+        tail = ref[feats : feats + TAIL, :].astype(F32)
+        return ref[0:feats, :].astype(F32), tail[0:1, :], tail[1:2, :]
+
+    def join_row(own, buf, sems, out, far, out_sem, far_sems, ident, ahead):
+        for j in range(share - 1):
+            whole(buf.at[j], sems.at[j]).wait()
+        parts = [opened(buf.at[j]) for j in range(share - 1)]
+        every = parts + [opened(own)]
+        lead_id = every[0][2]
+        for part in every[1:]:
+            lead_id = jnp.maximum(lead_id, part[2]) if ahead else jnp.minimum(lead_id, part[2])
+        sums = [jnp.where(p[2] == lead_id, p[0], 0.0) for p in every]
+        norms = [jnp.where(p[2] == lead_id, p[1], 0.0) for p in every]
+        total, end = payload(sum(sums), sum(norms), lead_id)
+        out[0:feats, :] = total
+        out[feats : feats + TAIL, :] = end
+        for k in range(2):
+            send(out, far.at[k], out_sem, far_sems.at[k], along(k + 1 if ahead else planes - 1 - k))
+        got, got_norm = jnp.zeros((feats, width), F32), jnp.zeros((1, feats), F32)
+        for j in range(share - 1):
+            source = lax.rem(col_x + share - 1 - j, share)
+            side = source < col_x if ahead else source > col_x
+            keep = (parts[j][2] == ident) & side
+            got += jnp.where(keep, parts[j][0], 0.0)
+            got_norm += jnp.where(keep, parts[j][1], 0.0)
+        back_s[...] = got
+        backn_s[...] = jnp.broadcast_to(got_norm, backn_s.shape)
+
+    def from_rows(far, far_sems, ident, ahead):
+        got, got_norm = back_s[...], backn_s[0:1, :]
+        for k in range(2):
+            whole(far.at[k], far_sems.at[k]).wait()
+            part = opened(far.at[k])
+            inside = row > k if ahead else row + k + 1 < planes
+            keep = (part[2] == ident) & inside
+            got += jnp.where(keep, part[0], 0.0)
+            got_norm += jnp.where(keep, part[1], 0.0)
+        return got, got_norm
+
+    for j in range(1, share):
+        send(sbuf, rbuf.at[j - 1], xs, xr.at[j - 1], beside(j))
+
+    def linear(h):
         q = qb[h]
         pre = dot_nn(q, fq[h])
         low = jnp.exp(jnp.minimum(pre, 0.0))
@@ -244,21 +268,36 @@
             score = dot_nt(phi[i:end], phik[0:end, :]) * mask[i:end, 0:end]
             num_s[h, i:end, :] = dot_nn(score.astype(BF16), vx[WIN : WIN + end, :])
             den_s[h, i:end, :] = jnp.sum(score, axis=1, keepdims=True)
-            for j in range(i, end, 128):
-                logits = dot_nt(q[j : j + 128], kx[j : j + 256, :]) * inv_scale
-                logits += bias[j : j + 128, :]
-                probs = jnp.exp(logits - jnp.max(logits, axis=1, keepdims=True))
-                total = jnp.sum(probs, axis=1, keepdims=True)
-                tea_s[h, j : j + 128, :] = dot_nn(probs.astype(BF16), vx[j : j + 256, :]) * (
-                    1.0 / total
-                )
+
+    def window(h):
+        q = qb[h]
+        for j in range(0, length, 128):
+            logits = dot_nt(q[j : j + 128], kx[j : j + 256, :]) * inv_scale
+            logits += bias[j : j + 128, :]
+            probs = jnp.exp(logits - jnp.max(logits, axis=1, keepdims=True))
+            total = jnp.sum(probs, axis=1, keepdims=True)
+            tea_s[h, j : j + 128, :] = dot_nn(probs.astype(BF16), vx[j : j + 256, :]) * (1.0 / total)
+
+    def forward(h, _):
+        whole(qb.at[h], qr.at[h]).wait()
+        linear(h)
+        window(h)
         return 0
 
-    lax.fori_loop(0, heads, forward, 0)
-
-    for k in range(REACH):
-        whole(rbuf.at[k], xr.at[k]).wait()
-    state, norm = gathered(rbuf, first_id, here, count, True)
+    for h in range(2):
+        whole(qb.at[h], qr.at[h]).wait()
+        linear(h)
+    for copy in rims:
+        copy.wait()
+    rim_f = jnp.where(here > 0, rim_in[...], -1).astype(F32)
+    bias[0:128, 0:128] = jnp.where((seg_col[0:128, :] == rim_f) & (c > r), 0.0, -1e30)
+
+    for h in range(2):
+        window(h)
+    lax.fori_loop(2, JOIN, forward, 0)
+    join_row(sbuf, rbuf, xr, ubuf, wbuf, us, ur, first_id, True)
+    lax.fori_loop(JOIN, heads, forward, 0)
+    state, norm = from_rows(wbuf, ur, first_id, True)
     state = state.astype(BF16)
 
     def meet(h, _):
@@ -286,43 +325,8 @@
     cbuf[0:feats, :] = total
     cbuf[feats : feats + TAIL, :] = end
 
-    def send(src, dst, send_sem, recv_sem, peer):
-        pltpu.make_async_remote_copy(
-            src_ref=src, dst_ref=dst, send_sem=send_sem, recv_sem=recv_sem,
-            device_id=peer, device_id_type=MESH,
-        ).start()
-
     for j in range(1, share):
         send(cbuf, dbuf.at[j - 1], cs, cr.at[j - 1], beside(j))
-
-    def opened(buf, slot):
-        tail = buf[slot, feats : feats + TAIL, :].astype(F32)
-        return buf[slot, 0:feats, :].astype(F32), tail[0:1, :], tail[1:2, :]
-
-    def join_row():
-        for j in range(share - 1):
-            whole(dbuf.at[j], cr.at[j]).wait()
-        parts = [opened(dbuf, j) for j in range(share - 1)]
-        mine_norm = cbuf[feats : feats + TAIL, :].astype(F32)
-        parts.append((cbuf[0:feats, :].astype(F32), mine_norm[0:1, :], mine_norm[1:2, :]))
-        lead_id = parts[0][2]
-        for part in parts[1:]:
-            lead_id = jnp.minimum(lead_id, part[2])
-        sums = [jnp.where(p[2] == lead_id, p[0], 0.0) for p in parts]
-        norms = [jnp.where(p[2] == lead_id, p[1], 0.0) for p in parts]
-        total, end = payload(sum(sums), sum(norms), lead_id)
-        tbuf[0:feats, :] = total
-        tbuf[feats : feats + TAIL, :] = end
-        for k in range(2):
-            send(tbuf, ebuf.at[k], es, er.at[k], along(planes - 1 - k))
-        back, back_norm = jnp.zeros((feats, width), F32), jnp.zeros((1, feats), F32)
-        for j in range(share - 1):
-            source = lax.rem(col_x + share - 1 - j, share)
-            keep = (parts[j][2] == last_id) & (source > col_x)
-            back += jnp.where(keep, parts[j][0], 0.0)
-            back_norm += jnp.where(keep, parts[j][1], 0.0)
-        back_s[...] = back
-        backn_s[...] = jnp.broadcast_to(back_norm, backn_s.shape)
 
     per = gq.shape[1]
 
@@ -371,10 +375,10 @@
         return backward(2 * t + 1, 0)
 
     lax.fori_loop(0, SPLIT // 2, backward_two, 0)
-    join_row()
     for turn in range(SPLIT):
         scatter(turn)
     backward_two(SPLIT // 2, 0)
+    join_row(cbuf, dbuf, cr, tbuf, ebuf, es, er, last_id, False)
     scatter(SPLIT)
     scatter(SPLIT + 1)
     backward_two(SPLIT // 2 + 1, 0)
@@ -383,13 +387,7 @@
     for turn in range(SPLIT - 1):
         climb(turn)
 
-    back, back_norm = back_s[...], backn_s[0:1, :]
-    for k in range(2):
-        whole(ebuf.at[k], er.at[k]).wait()
-        part = opened(ebuf, k)
-        keep = (part[2] == last_id) & (row + k + 1 < planes)
-        back += jnp.where(keep, part[0], 0.0)
-        back_norm += jnp.where(keep, part[1], 0.0)
+    back, back_norm = from_rows(ebuf, er, last_id, False)
     own = jnp.where(columns_of(seg_ref[...]) == last_id, 1.0, 0.0)
     d_phi = dphik[...] + own * (dot_nt(vx[WIN : WIN + length, 0:width], back.astype(BF16)) + back_norm)
     d_pre = (d_phi * slopek[...]).astype(BF16)
@@ -441,6 +439,8 @@
     for copy in sends:
         copy.wait_send()
     whole(qb.at[:, pl.ds(0, length - rows), :], qs).wait()
+    whole(rbuf, xs).wait()
+    whole(wbuf, us).wait()
     whole(dbuf, cs).wait()
     whole(ebuf, es).wait()
     whole(xin.at[:, pl.ds(0, share - 1)], s1).wait()
@@ -503,9 +503,11 @@
             pltpu.VMEM((width, feats), BF16),
             pltpu.VMEM((1, WIN), jnp.int32),
             pltpu.VMEM((packed, width), BF16),
-            pltpu.VMEM((REACH, packed, width), BF16),
+            pltpu.VMEM((share - 1, packed, width), BF16),
             pltpu.VMEM((packed, width), BF16),
             pltpu.VMEM((share - 1, packed, width), BF16),
+            pltpu.VMEM((packed, width), BF16),
+            pltpu.VMEM((2, packed, width), BF16),
             pltpu.VMEM((packed, width), BF16),
             pltpu.VMEM((2, packed, width), BF16),
             pltpu.VMEM((feats, width), F32),
@@ -547,10 +549,12 @@
             dma((heads,)),
             dma((3,)),
             dma((3,)),
-            dma((REACH,)),
-            dma((REACH,)),
             dma,
             dma((share - 1,)),
+            dma,
+            dma((share - 1,)),
+            dma,
+            dma((2,)),
             dma,
             dma((2,)),
         ]

time: 56.5 us -> 55.1 us (0.975)
  Pallas kernels: 55.3 us -> 54.3 us
    pallas_call x1, Pallas kernels: 54.1 us -> 53 us  [on_device(): pl.pallas_call(step_kernel, name='step', out_shape=(shape((length, heads...]
where the time goes in v5:
time: 55.1 us; the launch traced here: 55 us
  Pallas kernels  54.3 us (99%)
  between operations  0.64 us (1%)
    pallas_call x1, Pallas kernels, on_device(): pl.pallas_call(step_kernel, name='step', out_shape=(shape((length, heads...  53 us
    pallas_call x1, Pallas kernels, on_device(): pl.pallas_call(functools.partial(store_kernel, 1.0 / math.sqrt(length * c...  1.28 us

profile of v5, /device:TPU:2, one launch (start us, length us, event | category | flops | bytes accessed | tf_op | source)
XLA Modules:
  0.0 55.0 jit_solution(17746906137891644500)
XLA Ops:
  0.6 53.0 %step.1 = (bf16[512,1024]{1,0:T(8,128)(2,1)S(1)}, bf16[512,128]{1,0:T(8,128)(2,1)S(1)}, bf16[32,32,128]{2,1,0:T(8,128)(2,1)S(1)}, bf16[4,32,128]{2,1,0:T(8,128)(2,1)S(1)}) custom-call(bf16[128,4096]{1,0:T(8,128)(2,1)} %q_ref.1, bf16[128,512]{1,0:T(8,128)(2,1)} %k_ref.1, bf16[128,512]{1,0:T(8,128)(2,1)} %v_ref.1, s32[1,512]{1,0:T(1,128)} %bitcast.5, ...), custom_call_target="tpu_custom_call" | custom-call | tf_op jit(solution)/shard_map/step/pallas_call | solution.py:485
  53.7 1.3 %store.1 = (bf16[512,1024]{1,0:T(8,128)(2,1)}, bf16[512,128]{1,0:T(8,128)(2,1)}, f32[32,32,128]{2,1,0:T(8,128)}, f32[4,32,128]{2,1,0:T(8,128)}) custom-call(bf16[512,1024]{1,0:T(8,128)(2,1)S(1)} %get-tuple-element.12.err_in, bf16[512,128]{1,0:T(8,128)(2,1)S(1)} %get-tuple-element.13.keys_in, bf16[32,32,128]{2,1,0:T(8,128)(2,1)S(1)} %get-tuple-element.14.gq_in, ...), custom_call_target="tpu_custom_call" | custom-call | tf_op jit(solution)/shard_map/store/pallas_call | solution.py:569

commit v6 on v5

--- a/solution.py
+++ b/solution.py
@@ -296,7 +296,7 @@
         window(h)
     lax.fori_loop(2, JOIN, forward, 0)
     join_row(sbuf, rbuf, xr, ubuf, wbuf, us, ur, first_id, True)
-    lax.fori_loop(JOIN, heads, forward, 0)
+    lax.fori_loop(JOIN, heads - 2, forward, 0)
     state, norm = from_rows(wbuf, ur, first_id, True)
     state = state.astype(BF16)
 
@@ -320,7 +320,17 @@
         meet(2 * t, 0)
         return meet(2 * t + 1, 0)
 
-    lax.fori_loop(0, heads // 2, meet_two, 0)
+    def forward_meet(t, _):
+        h = heads - 2 + t
+        meet(2 * t, 0)
+        whole(qb.at[h], qr.at[h]).wait()
+        meet(2 * t + 1, 0)
+        linear(h)
+        window(h)
+        return 0
+
+    lax.fori_loop(0, 2, forward_meet, 0)
+    lax.fori_loop(2, heads // 2, meet_two, 0)
     total, end = payload(cot[...], jnp.sum(acc[...], axis=0, keepdims=True), first_id)
     cbuf[0:feats, :] = total
     cbuf[feats : feats + TAIL, :] = end
@@ -456,11 +466,21 @@
     whole(beyond, r7).wait()
 
 
-def store_kernel(scale, err_in, keys_in, gq_in, gk_in, err_out, keys_out, gq_out, gk_out):
-    err_out[...] = err_in[...]
-    keys_out[...] = keys_in[...]
-    gq_out[...] = gq_in[...].astype(F32) * scale
-    gk_out[...] = gk_in[...].astype(F32) * scale
+def store_kernel(scale, err_in, keys_in, gq_in, gk_in, err_out, keys_out, gq_out, gk_out, gq, gk, sem):
+    copies = [
+        pltpu.make_async_copy(err_in, err_out, sem.at[0]),
+        pltpu.make_async_copy(keys_in, keys_out, sem.at[1]),
+        pltpu.make_async_copy(gq, gq_out, sem.at[2]),
+        pltpu.make_async_copy(gk, gk_out, sem.at[3]),
+    ]
+    copies[0].start()
+    copies[1].start()
+    gk[...] = gk_in[...].astype(F32) * scale
+    copies[3].start()
+    gq[...] = gq_in[...].astype(F32) * scale
+    copies[2].start()
+    for copy in copies:
+        copy.wait()
 
 
 def on_device(queries, keys, values, segments, feat_q, feat_k):
@@ -576,7 +596,12 @@
             shape((share, width // share, feats), F32),
         ),
         in_specs=[vmem] * 4,
-        out_specs=[vmem] * 4,
+        out_specs=[hbm] * 4,
+        scratch_shapes=[
+            pltpu.VMEM((count, per, feats), F32),
+            pltpu.VMEM((share, width // share, feats), F32),
+            dma((4,)),
+        ],
         compiler_params=pltpu.CompilerParams(vmem_limit_bytes=8 * 1024 * 1024),
     )(*outs)
     return (

time: 55.1 us -> 54.8 us (level)
  no operation moved by 1% of the time
where the time goes in v6:
time: 54.8 us; the launch traced here: 54.7 us
  Pallas kernels  54 us (99%)
  between operations  0.64 us (1%)
    pallas_call x1, Pallas kernels, on_device(): pl.pallas_call(step_kernel, name='step', out_shape=(shape((length, heads...  52.8 us
    pallas_call x1, Pallas kernels, on_device(): pl.pallas_call(functools.partial(store_kernel, 1.0 / math.sqrt(length * c...  1.24 us

profile of v6, /device:TPU:2, one launch (start us, length us, event | category | flops | bytes accessed | tf_op | source)
XLA Modules:
  0.0 54.7 jit_solution(17666881162841007234)
XLA Ops:
  0.6 52.8 %step.1 = (bf16[512,1024]{1,0:T(8,128)(2,1)S(1)}, bf16[512,128]{1,0:T(8,128)(2,1)S(1)}, bf16[32,32,128]{2,1,0:T(8,128)(2,1)S(1)}, bf16[4,32,128]{2,1,0:T(8,128)(2,1)S(1)}) custom-call(bf16[128,4096]{1,0:T(8,128)(2,1)} %q_ref.1, bf16[128,512]{1,0:T(8,128)(2,1)} %k_ref.1, bf16[128,512]{1,0:T(8,128)(2,1)} %v_ref.1, s32[1,512]{1,0:T(1,128)} %bitcast.5, ...), custom_call_target="tpu_custom_call" | custom-call | tf_op jit(solution)/shard_map/step/pallas_call | solution.py:505
  53.4 1.2 %store.1 = (bf16[512,1024]{1,0:T(8,128)(2,1)}, bf16[512,128]{1,0:T(8,128)(2,1)}, f32[32,32,128]{2,1,0:T(8,128)}, f32[4,32,128]{2,1,0:T(8,128)}) custom-call(bf16[512,1024]{1,0:T(8,128)(2,1)S(1)} %get-tuple-element.12.err_in, bf16[512,128]{1,0:T(8,128)(2,1)S(1)} %get-tuple-element.13.keys_in, bf16[32,32,128]{2,1,0:T(8,128)(2,1)S(1)} %get-tuple-element.14.gq_in, ...), custom_call_target="tpu_custom_call" | custom-call | tf_op jit(solution)/shard_map/store/pallas_call | solution.py:589
